TPU v7x, 1024 devices: a whole 4x4x32 slice. The times are simulated.
1024 devices in a mesh: tensor: 16 (over y, x_hi, core), context: 64 (over x_lo, z).
Axes of the slice: x: 4 (x_hi: 2, x_lo: 2; x = x_hi * 2 + x_lo), y: 4, z: 32, core: 2. Of those that a mesh axis runs over, the one named last changes fastest.
Arguments:
- query: float32 [8192, 8192], P('context', 'tensor'), may hold values from -6 to 6
- keys: float32 [8192, 8192], P('context', 'tensor'), may hold values from -6 to 6
- values: float32 [8192, 8192], P('context', 'tensor'), may hold values from -6 to 6
- filters: float32 [8192, 512], P('context', 'tensor'), may hold values from -0.0625 to 0.0625
- w_out: bfloat16 [8192, 8192], P('tensor'), may hold values from -0.09375 to 0.09375
- grad_z: float32 [8192, 8192], P('context', 'tensor'), may hold values from -0.015625 to 0.015625
Outputs:
- out: float32 [8192, 8192], P('context', 'tensor')
- grad_filters: float32 [8192, 512], P('context', 'tensor')
All inputs are finite; a program needn't handle non-finite values.
Results may differ from a plain program's by a relative error of at most 0.009.
Values sent between devices are 32-bit elements; how exact they have to be, the bound alone decides.
No kernel may reach another device: no remote copies, remote signals or barrier semaphores. Data moves between devices by JAX's collectives and lax.ppermute only.
A program may use at most 64 MiB of HBM per device.

v0:
```python
import math

import jax
import jax.numpy as jnp
from jax import lax
from jax.sharding import PartitionSpec as P


def sent_together(arrays, axis, split_dim, concat_dim, along):
    both = jnp.concatenate(arrays, axis=along)
    whole, at, gathered = (
        lax.all_to_all(both, axis, split_axis=split_dim, concat_axis=concat_dim, tiled=True),
        0,
        [],
    )
    for a in arrays:
        gathered.append(lax.slice_in_dim(whole, at, at + a.shape[along], axis=along))
        at += a.shape[along]
    return tuple(gathered)


def angles(rows, cols, modulus):
    phase = rows[:, None] * cols[None, :] % modulus
    theta = phase.astype(jnp.float32) * (2.0 * math.pi / modulus)
    return (jnp.cos(theta), jnp.sin(theta))


def across(table, data):
    return jnp.einsum("ab,bjx->ajx", table, data, precision=lax.Precision.HIGHEST)


def across_back(table, data):
    return jnp.einsum("ba,bjx->ajx", table, data, precision=lax.Precision.HIGHEST)


def along(table, data):
    return jnp.einsum("mj,rjx->rmx", table, data, precision=lax.Precision.HIGHEST)


def on_device(query, keys, values, filters, w_out, grad_z):
    slab, chans = query.shape
    nfilt = filters.shape[1]
    group = chans // nfilt
    parts = lax.axis_size("context")
    piece = slab // parts
    total = 2 * parts * slab
    device = lax.axis_index("context")
    gated = keys * values
    backin = grad_z * query
    ex_gated, ex_back, ex_filt = sent_together(
        (
            gated.reshape(parts, piece, chans),
            backin.reshape(parts, piece, chans),
            filters.reshape(parts, piece, nfilt),
        ),
        "context",
        0,
        0,
        2,
    )
    order = jnp.arange(2 * parts, dtype=jnp.int32)
    owner = order // 2
    freq_rows = jnp.where(order % 2 == 0, owner, jnp.where(owner == 0, parts, 2 * parts - owner))
    cos_one, sin_one = angles(freq_rows, jnp.arange(parts, dtype=jnp.int32), 2 * parts)
    spec_re = across(cos_one, ex_gated) + across(sin_one, ex_back)
    spec_im = across(cos_one, ex_back) - across(sin_one, ex_gated)
    filt_re = across(cos_one, ex_filt)
    filt_im = -across(sin_one, ex_filt)
    local_pos = device * piece + jnp.arange(piece, dtype=jnp.int32)
    cos_tw, sin_tw = angles(freq_rows, local_pos, total)
    cos_tw = cos_tw[:, :, None]
    sin_tw = sin_tw[:, :, None]
    spec_re, spec_im = (spec_re * cos_tw + spec_im * sin_tw, spec_im * cos_tw - spec_re * sin_tw)
    filt_re, filt_im = (filt_re * cos_tw + filt_im * sin_tw, filt_im * cos_tw - filt_re * sin_tw)
    got_re, got_im, gfilt_re, gfilt_im = sent_together(
        (spec_re, spec_im, filt_re, filt_im), "context", 0, 1, 2
    )
    positions = jnp.arange(slab, dtype=jnp.int32)
    cos_two, sin_two = angles(positions, positions, slab)
    both_re = along(cos_two, got_re) + along(sin_two, got_im)
    both_im = along(cos_two, got_im) - along(sin_two, got_re)
    kern_re = along(cos_two, gfilt_re) + along(sin_two, gfilt_im)
    kern_im = along(cos_two, gfilt_im) - along(sin_two, gfilt_re)
    mirror_re = both_re[::-1, ::-1]
    mirror_im = both_im[::-1, ::-1]
    first_re = jnp.stack([jnp.roll(both_re[0, ::-1], 1, axis=0), both_re[1, ::-1]])
    first_im = jnp.stack([jnp.roll(both_im[0, ::-1], 1, axis=0), both_im[1, ::-1]])
    mirror_re = jnp.where(device == 0, first_re, mirror_re)
    mirror_im = jnp.where(device == 0, first_im, mirror_im)
    signal_re = 0.5 * (both_re + mirror_re)
    signal_im = 0.5 * (both_im - mirror_im)
    cotan_re = 0.5 * (both_im + mirror_im)
    cotan_im = -0.5 * (both_re - mirror_re)
    grouped = (2, slab, nfilt, group)
    signal_re = signal_re.reshape(grouped)
    signal_im = signal_im.reshape(grouped)
    cotan_re = cotan_re.reshape(grouped)
    cotan_im = cotan_im.reshape(grouped)
    kern_re = kern_re[..., None]
    kern_im = kern_im[..., None]
    conv_re = (kern_re * signal_re - kern_im * signal_im).reshape(2, slab, chans)
    conv_im = (kern_re * signal_im + kern_im * signal_re).reshape(2, slab, chans)
    dfilt_re = jnp.sum(cotan_re * signal_re + cotan_im * signal_im, axis=3)
    dfilt_im = jnp.sum(cotan_im * signal_re - cotan_re * signal_im, axis=3)
    mine = jnp.stack([device, jnp.where(device == 0, parts, 2 * parts - device)])
    cos_back, sin_back = angles(mine, positions, total)
    cos_back = cos_back[:, :, None]
    sin_back = sin_back[:, :, None]

    def inverse_local(real_part, imag_part):
        time_re = along(cos_two, real_part) - along(sin_two, imag_part)
        time_im = along(cos_two, imag_part) + along(sin_two, real_part)
        return (time_re * cos_back - time_im * sin_back, time_im * cos_back + time_re * sin_back)

    scale = 1.0 / total
    dfilt_re, dfilt_im = inverse_local(dfilt_re, dfilt_im)
    half = chans // 2
    pack_re = conv_re[..., :half] - conv_im[..., half:]
    pack_im = conv_im[..., :half] + conv_re[..., half:]
    pack_re, pack_im = inverse_local(pack_re, pack_im)
    back_re, back_im, bfilt_re, bfilt_im = sent_together(
        (pack_re, pack_im, dfilt_re, dfilt_im), "context", 1, 0, 2
    )
    lower = (across_back(cos_one, back_re) - across_back(sin_one, back_im)) * scale
    upper = (across_back(sin_one, back_re) + across_back(cos_one, back_im)) * scale
    conv_time = jnp.concatenate([lower, upper], axis=2)
    dfilt_time = (across_back(cos_one, bfilt_re) - across_back(sin_one, bfilt_im)) * scale
    conv_slab, dfilt_slab = (
        lax.all_to_all(conv_time, "context", split_axis=0, concat_axis=1, tiled=True),
        lax.all_to_all(dfilt_time, "context", split_axis=0, concat_axis=1, tiled=True),
    )
    conv = conv_slab.reshape(slab, chans)
    mixed = (query * conv).astype(jnp.bfloat16)
    summed = lax.psum_scatter(
        lax.dot_general(w_out, mixed, (((0,), (1,)), ((), ())), preferred_element_type=jnp.float32),
        "tensor",
        scatter_dimension=0,
        tiled=True,
    )
    return (summed.T, dfilt_slab.reshape(slab, nfilt))


def solution(mesh):
    placed = (
        P("context", "tensor"),
        P("context", "tensor"),
        P("context", "tensor"),
        P("context", "tensor"),
        P("tensor", None),
        P("context", "tensor"),
    )
    return jax.shard_map(
        on_device,
        mesh=mesh,
        in_specs=placed,
        out_specs=(P("context", "tensor"), P("context", "tensor")),
        check_vma=False,
    )
```

profile of v0, /device:TPU:1, one launch (start us, length us, event | category | flops | bytes accessed | tf_op | source)
XLA Modules:
  0.0 521.9 jit_solution(5058816498739133878)
XLA Ops:
  7.2 0.8 copy.63
  8.0 1.1 mul.528
  9.2 1.1 mul.529
  10.4 1.1 pad_maximum_fusion
  11.5 30.8 %all-to-all-start = ((f32[64,2,1056]{2,1,0:T(2,128)}), f32[64,2,1056]{2,1,0:T(2,128)S(1)}, u32[]{:S(2)}, u32[]{:S(2)}) async-start(f32[64,2,1056]{2,1,0:T(2,128)} %pad_maximum_fusion), calls=%async_computation | async-start | bytes 1179648 | tf_op jit(solution)/shard_map/all_to_all | solution.py:12
  42.5 60.3 %all-to-all-done = f32[64,2,1056]{2,1,0:T(2,128)S(1)} async-done(((f32[64,2,1056]{2,1,0:T(2,128)}), f32[64,2,1056]{2,1,0:T(2,128)S(1)}, u32[]{:S(2)}, u32[]{:S(2)}) %all-to-all-start) | async-done | bytes 540704 | tf_op jit(solution)/shard_map/all_to_all | solution.py:12
  103.8 0.8 fusion.18
  104.6 0.8 fusion.14
  105.3 0.8 convolution_subtract_fusion
  106.1 0.9 multiply_subtract_fusion.1
  107.3 1.9 copy.69
  109.2 13.7 %all-to-all-start.1 = ((f32[128,2,1088]{2,1,0:T(2,128)}), f32[128,2,1088]{2,1,0:T(2,128)S(1)}, u32[]{:S(2)}, u32[]{:S(2)}) async-start(f32[128,2,1088]{2,1,0:T(2,128)} %copy.69), calls=%async_computation.1 | async-start | bytes 2359296 | tf_op jit(solution)/shard_map/all_to_all | solution.py:12
  123.4 99.1 %all-to-all-done.1 = f32[128,2,1088]{2,1,0:T(2,128)S(1)} async-done(((f32[128,2,1088]{2,1,0:T(2,128)}), f32[128,2,1088]{2,1,0:T(2,128)S(1)}, u32[]{:S(2)}, u32[]{:S(2)}) %all-to-all-start.1) | async-done | bytes 1114144 | tf_op jit(solution)/shard_map/all_to_all | solution.py:12
  222.5 0.6 copy.70
  224.2 0.8 fusion.39
  225.0 0.8 fusion.43
  225.8 0.8 fusion.1
  226.8 0.7 slice_bitcast_fusion.1
  227.6 0.8 fusion
  228.5 0.7 slice_bitcast_fusion
  229.3 0.7 rev.15
  230.0 0.7 rev.17
  230.8 0.5 fusion.41
  231.3 0.5 fusion.45
  231.8 0.5 fusion.4
  232.3 0.5 fusion.5
  233.9 1.5 slice.107
  235.4 1.3 maximum_bitcast_fusion
  237.0 0.4 bitcast_reduce_fusion
  237.6 0.6 fusion.21
  238.2 0.6 fusion.20
  238.8 0.5 fusion.33
  239.3 0.5 fusion.35
  239.8 0.5 convolution_add_fusion.4
  240.2 0.6 convolution_add_fusion.2
  240.9 0.5 subtract_bitcast_fusion.1
  241.4 0.6 subtract_bitcast_fusion
  242.1 0.8 copy.75
  242.9 91.0 %all_to_all.59 = f32[2,128,576]{2,0,1:T(2,128)S(1)} all-to-all(f32[2,128,576]{2,0,1:T(2,128)S(1)} %copy.75), channel_id=1, replica_groups=mesh['tensor'=16,'context'=64] {'context'}, dimensions={1} | all-to-all | bytes 1179648 | tf_op jit(solution)/shard_map/all_to_all | solution.py:12
  334.4 0.4 fusion.10
  334.8 0.4 fusion.12
  335.3 0.4 fusion.3
  335.7 0.4 fusion.2
  336.4 51.0 %all_to_all.60 = f32[64,2,512]{2,1,0:T(2,128)S(1)} all-to-all(f32[64,2,512]{2,1,0:T(2,128)S(1)} %copy.79), channel_id=1, replica_groups=mesh['tensor'=16,'context'=64] {'context'}, dimensions={0} | all-to-all | bytes 524288 | tf_op jit(solution)/shard_map/all_to_all | solution.py:129
  387.6 6.6 %convolution_bitcast_fusion = f32[8192,128]{0,1:T(8,128)} fusion(bf16[512,8192]{1,0:T(8,128)(2,1)} %param.10, f32[128,512]{1,0:T(8,128)S(1)} %copy-done, f32[128,512]{1,0:T(8,128)S(1)} %reshape.202), kind=kOutput, calls=%fused_computation | convolution fusion | flops 1073872896 | bytes 13107200 | tf_op jit(solution)/shard_map/dot_general | solution.py:135
  395.3 32.1 %all_to_all.61 = f32[64,2,32]{2,1,0:T(2,128)S(1)} all-to-all(f32[64,2,32]{2,1,0:T(2,128)S(1)} %copy.82), channel_id=1, replica_groups=mesh['tensor'=16,'context'=64] {'context'}, dimensions={0} | all-to-all | bytes 32768 | tf_op jit(solution)/shard_map/all_to_all | solution.py:130
  427.5 0.7 copy.83
  428.2 86.9 %reduce-scatter.2.cloned.1.call-done = f32[512,128]{0,1:T(8,128)} async-done(((f32[8192,128]{0,1:T(8,128)}), f32[512,128]{0,1:T(8,128)}) %reduce-scatter.2.cloned.1.call-update) | async-done | bytes 262160 | tf_op jit(solution)/shard_map/reduce_scatter | solution.py:134
  (48 shorter events, 7.1 us)
Async XLA Ops:
  11.5 91.3 %all-to-all-start = ((f32[64,2,1056]{2,1,0:T(2,128)}), f32[64,2,1056]{2,1,0:T(2,128)S(1)}, u32[]{:S(2)}, u32[]{:S(2)}) async-start(f32[64,2,1056]{2,1,0:T(2,128)} %pad_maximum_fusion), calls=%async_computation | async-start | bytes 1179648 | tf_op jit(solution)/shard_map/all_to_all | solution.py:12
  109.2 113.3 %all-to-all-start.1 = ((f32[128,2,1088]{2,1,0:T(2,128)}), f32[128,2,1088]{2,1,0:T(2,128)S(1)}, u32[]{:S(2)}, u32[]{:S(2)}) async-start(f32[128,2,1088]{2,1,0:T(2,128)} %copy.69), calls=%async_computation.1 | async-start | bytes 2359296 | tf_op jit(solution)/shard_map/all_to_all | solution.py:12
  123.0 392.1 %reduce-scatter.2.cloned.1.call-start = ((), (), s32[]{:S(2)}) async-start(), calls=%async_computation.6 | async-start | bytes 4456448 | tf_op jit(solution)/shard_map/reduce_scatter | solution.py:134
  242.1 145.5 %copy-start = (f32[128,512]{1,0:T(8,128)S(1)}, f32[128,512]{1,0:T(8,128)}, u32[]{:S(2)}) copy-start(f32[128,512]{1,0:T(8,128)} %param.6) | copy-start | bytes 786436
Sparse Core Ops, SparseCore 0:
  394.3 120.7 reduce-scatter.1
where the time goes:
time: 523 us; the launch traced here: 522 us
  waiting for transfers between devices  246 us (47%)
  blocking collectives  174 us (33%)
  starting transfers between devices  44.8 us (9%)
  matrix products  22.4 us (4%)
  between operations  14.5 us (3%)
  local copies, waits for them, and re-layouts  14.1 us (3%)
  other arithmetic  5.72 us (1%)
    all_to_all x2, waiting for transfers between devices, sent_together(): lax.all_to_all(both, axis, split_axis=split_dim, concat_axis=concat_dim,...  159 us
    all_to_all x1, blocking collectives, sent_together(): lax.all_to_all(both, axis, split_axis=split_dim, concat_axis=concat_dim,...  91 us
    reduce_scatter x1, waiting for transfers between devices, on_device(): lax.psum_scatter(lax.dot_general(w_out, mixed, (((0,), (1,)), ((), ())),...  86.9 us
    all_to_all x1, blocking collectives, on_device(): lax.all_to_all(conv_time, 'context', split_axis=0, concat_axis=1, tiled=T...  51 us
    all_to_all x2, starting transfers between devices, sent_together(): lax.all_to_all(both, axis, split_axis=split_dim, concat_axis=concat_dim,...  44.5 us
    all_to_all x1, blocking collectives, on_device(): lax.all_to_all(dfilt_time, 'context', split_axis=0, concat_axis=1, tiled=...  32.1 us
  transfers between devices with their start and end apart: 3, of which 3 were waited for; matrix products, arithmetic and copies ran while one was open for 0% of the time, Pallas kernels for 0%

commit v1 on v0

v1 whole, which is shorter than its diff:
```python
import jax
import jax.numpy as jnp
import numpy as np
from jax import lax
from jax.experimental import pallas as pl
from jax.experimental.pallas import tpu as pltpu
from jax.sharding import Mesh, PartitionSpec as P

FINE = (("y", 4), ("xh", 2), ("core", 2), ("xl", 2), ("z", 32))
TENSOR = ("y", "xh", "core")
CONTEXT = ("xl", "z")
ROWS = 8
B = 128
F32 = jnp.float32
BF16 = jnp.bfloat16
VMEM = pl.BlockSpec(memory_space=pltpu.VMEM)


def gate_kernel(q_ref, k_ref, v_ref, f_ref, z_ref, out_ref):
    n = out_ref.shape[0]
    gated = (k_ref[...] * v_ref[...]).T
    backin = (z_ref[...] * q_ref[...]).T
    filt = f_ref[...]
    out_ref[:, 0:ROWS, :] = gated.reshape(n, ROWS, B)
    out_ref[:, ROWS : 2 * ROWS, :] = backin.reshape(n, ROWS, B)
    share = n // filt.shape[0]
    for j in range(n):
        out_ref[j, 2 * ROWS : 2 * ROWS + 1, :] = filt[j // share : j // share + 1, :]


def gate(q, k, v, f, z, parts):
    return pl.pallas_call(
        gate_kernel,
        out_shape=jax.ShapeDtypeStruct((parts, 2 * ROWS + 1, B), F32),
        in_specs=[VMEM] * 5,
        out_specs=VMEM,
        name="gate",
    )(q, k, v, f.T, z)


def wide(x):
    x = x.reshape(x.shape[0] // 2, 2, ROWS, B)
    return jnp.concatenate([x[:, 0], x[:, 1]], axis=-1).reshape(-1, 2 * B)


def conv_kernel(in_ref, out_ref, filt_ref, toep_ref, pad_ref, flip_ref, acc_ref, outer_ref, pos_ref, neg_ref):
    nb = in_ref.shape[0]
    half = nb // 2
    rows = half * ROWS
    row = lax.broadcasted_iota(jnp.int32, (B, B), 0)
    lane = lax.broadcasted_iota(jnp.int32, (B, B), 1)
    for j in range(nb):
        filt_ref[j : j + 1, :] = in_ref[j, 2 * ROWS : 2 * ROWS + 1, :]
    toep_ref[nb * B : (nb + 1) * B, :] = jnp.zeros((B, B), BF16)

    def build(dist, before):
        taps = jnp.broadcast_to(filt_ref[pl.ds(dist, 1), :], (B, B))
        now = pltpu.roll(taps, 0, 1, stride=1, stride_axis=0)
        at = pl.multiple_of((nb - 1 - dist) * B, B)
        toep_ref[pl.ds(at, B), :] = jnp.where(lane >= row, now, before).astype(BF16)
        return now

    lax.fori_loop(0, nb, build, jnp.zeros((B, B), F32), unroll=4)

    pad_ref[0:rows, :] = jnp.zeros((rows, 2 * B), F32)
    gated = wide(in_ref[:, 0:ROWS, :])
    pad_ref[rows : 2 * rows, :] = gated
    flip = jnp.where(lane + row == B - 1, 1.0, 0.0).astype(BF16)
    flip_ref[0:rows, :] = jnp.zeros((rows, 2 * B), F32)
    for p in range(2):
        part = gated[:, p * B : (p + 1) * B].astype(BF16)
        flip_ref[rows : 2 * rows, p * B : (p + 1) * B] = jnp.dot(part, flip, preferred_element_type=F32)
    back_t = wide(in_ref[:, ROWS : 2 * ROWS, :]).T.astype(BF16)
    acc_ref[...] = jnp.zeros((rows, 2 * B), F32)

    def step(d, carried):
        start = pl.multiple_of(rows - ROWS * d, ROWS)
        shifted = pad_ref[pl.ds(start, rows), :].astype(BF16)
        even = pl.multiple_of((nb - 1 - 2 * d) * B, B)
        odd = pl.multiple_of((nb - 2 - 2 * d) * B, B)
        taps = jnp.concatenate([toep_ref[pl.ds(even, 2 * B), :], toep_ref[pl.ds(odd, 2 * B), :]], axis=1)
        acc_ref[...] += jnp.dot(shifted, taps, preferred_element_type=F32)
        flipped = flip_ref[pl.ds(start, rows), :].astype(BF16)
        outer = jnp.dot(back_t, flipped, preferred_element_type=F32)
        outer_ref[2 * d] = carried + outer[0:B, B : 2 * B]
        outer_ref[2 * d + 1] = outer[0:B, 0:B] + outer[B : 2 * B, B : 2 * B]
        return outer[B : 2 * B, 0:B]

    outer_ref[nb] = lax.fori_loop(0, half, step, jnp.zeros((B, B), F32), unroll=2)

    later = (lane < row) | (lane == B - 1)

    def diagonals(dist, _):
        rolled = pltpu.roll(outer_ref[dist + 1], 0, 1, stride=1, stride_axis=0)
        kept = jnp.where(later, rolled, 0.0)
        pos_ref[pl.ds(dist, 1), :] = jnp.sum(kept, axis=0, keepdims=True)
        neg_ref[pl.ds(dist, 1), :] = jnp.sum(rolled - kept, axis=0, keepdims=True)
        return 0

    lax.fori_loop(0, nb, diagonals, 0, unroll=4)
    neg_ref[nb : nb + 1, :] = jnp.zeros((1, B), F32)
    turned = pos_ref[...] + neg_ref[1 : nb + 1, :]
    pos_ref[...] = pltpu.roll(turned, 1, 1)
    for p in range(2):
        out_ref[:, p, 0:ROWS, :] = acc_ref[:, p * B : (p + 1) * B].reshape(half, ROWS, B)
    for j in range(nb):
        out_ref[j // 2, j % 2, ROWS : ROWS + 1, :] = pos_ref[j : j + 1, :]


def convolve(x):
    nb = x.shape[0]
    half = nb // 2
    y = pl.pallas_call(
        conv_kernel,
        out_shape=jax.ShapeDtypeStruct((half, 2, ROWS + 1, B), F32),
        in_specs=[VMEM],
        out_specs=VMEM,
        scratch_shapes=[
            pltpu.VMEM((nb, B), F32),
            pltpu.VMEM(((nb + 1) * B, B), BF16),
            pltpu.VMEM((2 * half * ROWS, 2 * B), F32),
            pltpu.VMEM((2 * half * ROWS, 2 * B), F32),
            pltpu.VMEM((half * ROWS, 2 * B), F32),
            pltpu.VMEM((nb + 1, B, B), F32),
            pltpu.VMEM((nb, B), F32),
            pltpu.VMEM((nb + 8, B), F32),
        ],
        name="conv",
    )(x)
    return y.reshape(nb, ROWS + 1, B)


def first_kernel(core_ref, q_ref, c_ref, w_ref, out_ref, mixed_ref):
    @pl.when(pl.program_id(0) == 0)
    def _():
        conv = c_ref[:, 0:ROWS, :].reshape(-1, B).T
        mixed_ref[...] = (q_ref[...] * conv).astype(BF16)

    out_ref[0] = jnp.dot(mixed_ref[...], w_ref[...], preferred_element_type=F32)


def second_kernel(core_ref, mixed_ref, w_ref, out_ref):
    out_ref[0] = jnp.dot(mixed_ref[...], w_ref[...], preferred_element_type=F32)


def project(q, c, w, core, n):
    slab, chans = q.shape
    wide_n = w.shape[1] // n
    pairs = n // 2
    cost = pl.CostEstimate(flops=slab * chans * w.shape[1], bytes_accessed=w.size, transcendentals=0)
    out = jax.ShapeDtypeStruct((pairs, slab, wide_n), F32)
    out_spec = pl.BlockSpec((1, slab, wide_n), lambda i, s: (i, 0, 0))
    w_spec = pl.BlockSpec((chans, wide_n), lambda i, s: (0, 2 * i + s[0]))

    def fixed(shape):
        return pl.BlockSpec(shape, lambda i, s: (0,) * len(shape))

    theirs, mixed = pl.pallas_call(
        first_kernel,
        out_shape=(out, jax.ShapeDtypeStruct((slab, chans), BF16)),
        grid_spec=pltpu.PrefetchScalarGridSpec(
            num_scalar_prefetch=1,
            grid=(pairs,),
            in_specs=[fixed(q.shape), fixed(c.shape), w_spec],
            out_specs=(out_spec, fixed((slab, chans))),
        ),
        cost_estimate=cost,
        name="theirs",
    )((1 - core).reshape(1), q, c, w)
    mine = pl.pallas_call(
        second_kernel,
        out_shape=out,
        grid_spec=pltpu.PrefetchScalarGridSpec(
            num_scalar_prefetch=1,
            grid=(pairs,),
            in_specs=[fixed((slab, chans)), w_spec],
            out_specs=out_spec,
        ),
        cost_estimate=cost,
        name="mine",
    )(core.reshape(1), mixed, w)
    return theirs, mine


def on_device(query, keys, values, filters, w_out, grad_z):
    parts = lax.axis_size(CONTEXT)
    n = lax.axis_size(TENSOR)
    nfilt = filters.shape[1]
    core = lax.axis_index("core").astype(jnp.int32)
    sent = gate(query, keys, values, filters, grad_z, parts)
    whole = lax.all_to_all(sent, CONTEXT, split_axis=0, concat_axis=0, tiled=True)
    result = convolve(whole)
    back = lax.all_to_all(result, CONTEXT, split_axis=0, concat_axis=0, tiled=True)
    theirs, mine = project(query, back, w_out, core, n)
    swapped = lax.ppermute(theirs, "core", [(0, 1), (1, 0)])
    grad_filters = back[:, ROWS, :].reshape(nfilt, parts // nfilt, B).sum(axis=1).T
    summed = mine + swapped
    pieces = lax.all_to_all(summed, ("y", "xh"), split_axis=0, concat_axis=0, tiled=True)
    return jnp.sum(pieces, axis=0), grad_filters


def solution(mesh):
    fine = Mesh(
        np.asarray(mesh.devices).reshape([size for _, size in FINE]),
        [name for name, _ in FINE],
    )
    both = P(CONTEXT, TENSOR)
    return jax.shard_map(
        on_device,
        mesh=fine,
        in_specs=(both, both, both, both, P(TENSOR, None), both),
        out_specs=(both, both),
        check_vma=False,
    )
```

time: 523 us -> 254 us (0.49)
  waiting for transfers between devices: 246 us -> 82.5 us
  blocking collectives: 174 us -> 105 us
  Pallas kernels: 0 us -> 27.9 us
  matrix products: 22.4 us -> 0 us
  starting transfers between devices: 44.8 us -> 28.4 us
  between operations: 14.5 us -> 0.66 us
  local copies, waits for them, and re-layouts: 14.1 us -> 1.76 us
    reduce_scatter x1 -> x0, waiting for transfers between devices: 86.9 us -> none  [on_device(): lax.psum_scatter(lax.dot_general(w_out, mixed, (((0,), (1,)), ((), ())),...]
    all_to_all x2, waiting for transfers between devices: 159 us -> 82.5 us  [the longest x1 55.8 us: on_device(): lax.all_to_all(result, CONTEXT, split_axis=0, concat_axis=0, tiled=True)]
    all_to_all x3 -> x1, blocking collectives: 174 us -> 105 us  [on_device(): lax.all_to_all(sent, CONTEXT, split_axis=0, concat_axis=0, tiled=True)]
    pallas_call x0 -> x4, Pallas kernels: none -> 27.9 us  [the longest x1 11.5 us: convolve(): pl.pallas_call(conv_kernel, out_shape=jax.ShapeDtypeStruct((half, 2, ROWS...]
    all_to_all x2, starting transfers between devices: 44.5 us -> 23.3 us  [the longest x1 16.9 us: on_device(): lax.all_to_all(result, CONTEXT, split_axis=0, concat_axis=0, tiled=True)]
    dot_general x25 -> x0, matrix products: 21.1 us -> none  [the longest x16 9.61 us: along(): jnp.einsum('mj,rjx->rmx', table, data, precision=lax.Precision.HIGHEST)]
  transfers between devices with their start and end apart: 3 -> 3, of which waited for: 3 -> 2; matrix products, arithmetic and copies ran while one was open for 0% -> 1% of each run, Pallas kernels for 0% -> 3%
where the time goes in v1:
time: 254 us; the launch traced here: 252 us
  blocking collectives  105 us (41%)
  waiting for transfers between devices  82.5 us (32%)
  starting transfers between devices  28.4 us (11%)
  Pallas kernels  27.9 us (11%)
  other arithmetic  4.93 us (2%)
    all_to_all x1, blocking collectives, on_device(): lax.all_to_all(sent, CONTEXT, split_axis=0, concat_axis=0, tiled=True)  105 us
    all_to_all x1, waiting for transfers between devices, on_device(): lax.all_to_all(result, CONTEXT, split_axis=0, concat_axis=0, tiled=True)  55.8 us
    all_to_all x1, waiting for transfers between devices, on_device(): lax.all_to_all(summed, ('y', 'xh'), split_axis=0, concat_axis=0, tiled=True)  26.6 us
    all_to_all x1, starting transfers between devices, on_device(): lax.all_to_all(result, CONTEXT, split_axis=0, concat_axis=0, tiled=True)  16.9 us
    pallas_call x1, Pallas kernels, convolve(): pl.pallas_call(conv_kernel, out_shape=jax.ShapeDtypeStruct((half, 2, ROWS...  11.5 us
    pallas_call x1, Pallas kernels, project(): pl.pallas_call(first_kernel, out_shape=(out, jax.ShapeDtypeStruct((slab,...  7.2 us
    pallas_call x1, Pallas kernels, project(): pl.pallas_call(second_kernel, out_shape=out, grid_spec=pltpu.PrefetchScal...  6.92 us
    all_to_all x1, starting transfers between devices, on_device(): lax.all_to_all(summed, ('y', 'xh'), split_axis=0, concat_axis=0, tiled=True)  6.4 us
  transfers between devices with their start and end apart: 3, of which 2 were waited for; matrix products, arithmetic and copies ran while one was open for 1% of the time, Pallas kernels for 3%

profile of v1, /device:TPU:1, one launch (start us, length us, event | category | flops | bytes accessed | tf_op | source)
XLA Modules:
  0.0 251.6 jit_solution(6234977152479820835)
XLA Ops:
  0.6 2.3 gate.1
  2.9 105.4 %all_to_all.15.in_ref = f32[64,17,128]{2,1,0:T(8,128)} all-to-all(f32[64,17,128]{2,1,0:T(8,128)} %gate.1), channel_id=1, replica_groups=mesh['y'=4,'xh'=2,'core'=2,'xl'=2,'z'=32] {'xl','z'}, dimensions={0} | all-to-all | bytes 1114112 | tf_op jit(solution)/shard_map/all_to_all | solution.py:191
  108.3 11.5 %conv.1 = f32[32,2,9,128]{3,2,1,0:T(8,128)} custom-call(f32[64,17,128]{2,1,0:T(8,128)} %all_to_all.15.in_ref), custom_call_target="tpu_custom_call" | custom-call | tf_op jit(solution)/shard_map/conv/pallas_call | solution.py:113
  119.9 16.9 %all-to-all-start.1 = ((f32[64,9,128]{2,1,0:T(8,128)}), f32[64,9,128]{2,1,0:T(8,128)S(1)}, u32[]{:S(2)}, u32[]{:S(2)}) async-start(f32[64,9,128]{2,1,0:T(8,128)} %bitcast.6), calls=%async_computation.1 | async-start | bytes 1048576 | tf_op jit(solution)/shard_map/all_to_all | solution.py:193
  136.8 55.8 %all-to-all-done.1.c_ref = f32[64,9,128]{2,1,0:T(8,128)S(1)} async-done(((f32[64,9,128]{2,1,0:T(8,128)}), f32[64,9,128]{2,1,0:T(8,128)S(1)}, u32[]{:S(2)}, u32[]{:S(2)}) %all-to-all-start.1) | async-done | bytes 294944 | tf_op jit(solution)/shard_map/all_to_all | solution.py:193
  192.6 0.0 copy-start
  192.6 0.8 copy-done
  193.4 7.2 %theirs.1 = (f32[8,128,512]{2,1,0:T(8,128)}, bf16[128,512]{1,0:T(8,128)(2,1)}) custom-call(s32[1]{0:T(128)} %bitcast.1.core_ref, f32[128,512]{1,0:T(8,128)} %q_ref.3, f32[64,9,128]{2,1,0:T(8,128)} %copy-done, bf16[512,8192]{1,0:T(8,128)(2,1)} %w_ref.3), custom_call_target="tpu_custom_call" | custom-call | flops 536870912 | bytes 4194304 | tf_op jit(solution)/shard_map/theirs/pallas_call | solution.py:158
  200.6 5.1 %collective-permute-start = (f32[8,128,512]{2,1,0:T(8,128)}, f32[8,128,512]{2,1,0:T(8,128)S(1)}, u32[]{:S(2)}, u32[]{:S(2)}) collective-permute-start(f32[8,128,512]{2,1,0:T(8,128)} %get-tuple-element.5), channel_id=1, source_target_pairs={{0,64},{64,0},{1,65},{65,1},{2,66},{66,2},{3,67},{67,3},{4,68},{68... | collective-permute-start | bytes 6291464 | tf_op jit(solution)/shard_map/ppermute | solution.py:195
  205.7 6.9 %mine.1 = f32[8,128,512]{2,1,0:T(8,128)} custom-call(s32[1]{0:T(128)} %bitcast.core_ref, bf16[128,512]{1,0:T(8,128)(2,1)} %get-tuple-element.4.mixed_ref, bf16[512,8192]{1,0:T(8,128)(2,1)} %w_ref.3), custom_call_target="tpu_custom_call" | custom-call | flops 536870912 | bytes 4194304 | tf_op jit(solution)/shard_map/mine/pallas_call | solution.py:170
  212.6 0.0 collective-permute-done
  212.6 3.4 %add.3 = f32[8,128,512]{2,1,0:T(8,128)} add(f32[8,128,512]{2,1,0:T(8,128)} %mine.1, f32[8,128,512]{2,1,0:T(8,128)S(1)} %collective-permute-done) | non-fusion elementwise | flops 524288 | bytes 6291456 | tf_op jit(solution)/shard_map/add | solution.py:197
  216.0 6.4 %all-to-all-start.2 = ((f32[8,128,512]{2,1,0:T(8,128)}), f32[8,128,512]{2,1,0:T(8,128)S(1)}, u32[]{:S(2)}, u32[]{:S(2)}) async-start(f32[8,128,512]{2,1,0:T(8,128)} %add.3), calls=%async_computation.2 | async-start | bytes 4194304 | tf_op jit(solution)/shard_map/all_to_all | solution.py:198
  222.4 1.0 slice.4
  223.4 0.6 reduce_sum.19
  224.0 26.6 %all-to-all-done.2 = f32[8,128,512]{2,1,0:T(8,128)S(1)} async-done(((f32[8,128,512]{2,1,0:T(8,128)}), f32[8,128,512]{2,1,0:T(8,128)S(1)}, u32[]{:S(2)}, u32[]{:S(2)}) %all-to-all-start.2) | async-done | bytes 2097184 | tf_op jit(solution)/shard_map/all_to_all | solution.py:198
  250.6 0.9 reduce_sum.18
Async XLA Ops:
  119.9 72.8 %all-to-all-start.1 = ((f32[64,9,128]{2,1,0:T(8,128)}), f32[64,9,128]{2,1,0:T(8,128)S(1)}, u32[]{:S(2)}, u32[]{:S(2)}) async-start(f32[64,9,128]{2,1,0:T(8,128)} %bitcast.6), calls=%async_computation.1 | async-start | bytes 1048576 | tf_op jit(solution)/shard_map/all_to_all | solution.py:193
  192.6 0.8 copy-start
  200.6 12.0 %collective-permute-start = (f32[8,128,512]{2,1,0:T(8,128)}, f32[8,128,512]{2,1,0:T(8,128)S(1)}, u32[]{:S(2)}, u32[]{:S(2)}) collective-permute-start(f32[8,128,512]{2,1,0:T(8,128)} %get-tuple-element.5), channel_id=1, source_target_pairs={{0,64},{64,0},{1,65},{65,1},{2,66},{66,2},{3,67},{67,3},{4,68},{68... | collective-permute-start | bytes 6291464 | tf_op jit(solution)/shard_map/ppermute | solution.py:195
  216.0 34.6 %all-to-all-start.2 = ((f32[8,128,512]{2,1,0:T(8,128)}), f32[8,128,512]{2,1,0:T(8,128)S(1)}, u32[]{:S(2)}, u32[]{:S(2)}) async-start(f32[8,128,512]{2,1,0:T(8,128)} %add.3), calls=%async_computation.2 | async-start | bytes 4194304 | tf_op jit(solution)/shard_map/all_to_all | solution.py:198

commit v2 on v1

v2 whole, which is shorter than its diff:
```python
import jax
import jax.numpy as jnp
import numpy as np
from jax import lax
from jax.experimental import pallas as pl
from jax.experimental.pallas import tpu as pltpu
from jax.sharding import Mesh, PartitionSpec as P

FINE = (("y", 4), ("xh", 2), ("core", 2), ("xl", 2), ("z", 32))
TENSOR = ("y", "xh", "core")
CONTEXT = ("xl", "z")
ROWS = 8
B = 128
F32 = jnp.float32
BF16 = jnp.bfloat16
VMEM = pl.BlockSpec(memory_space=pltpu.VMEM)
HBM = pl.BlockSpec(memory_space=pltpu.HBM)


def params(mib):
    return pltpu.CompilerParams(vmem_limit_bytes=mib << 20)


def gate_kernel(q_hbm, k_hbm, v_hbm, z_hbm, f_hbm, out_ref, in_ref, f_ref, turn_ref, sem):
    width = 2 * ROWS + 1
    n = out_ref.shape[0] // width
    share = n // f_ref.shape[0]
    copies = [pltpu.make_async_copy(f_hbm, f_ref, sem.at[4])]
    for i, hbm in enumerate((k_hbm, v_hbm, z_hbm, q_hbm)):
        copies.append(pltpu.make_async_copy(hbm, in_ref.at[i], sem.at[i]))
    for copy in copies:
        copy.start()
    copies[0].wait()
    for r in range(share):
        out_ref[pl.ds(r * width + 2 * ROWS, n // share, stride=share * width), :] = f_ref[...]
    for i in range(2):
        copies[2 * i + 1].wait()
        copies[2 * i + 2].wait()
        turn_ref[i] = (in_ref[2 * i] * in_ref[2 * i + 1]).T
        for r in range(ROWS):
            rows = turn_ref[i, pl.ds(r, n, stride=ROWS), :]
            out_ref[pl.ds(i * ROWS + r, n, stride=width), :] = rows


def gate(q, k, v, f, z, parts):
    return pl.pallas_call(
        gate_kernel,
        out_shape=jax.ShapeDtypeStruct((parts * (2 * ROWS + 1), B), F32),
        in_specs=[HBM] * 5,
        out_specs=VMEM,
        scratch_shapes=[
            pltpu.VMEM((4,) + q.shape, F32),
            pltpu.VMEM(f.shape[::-1], F32),
            pltpu.VMEM((2, q.shape[1], B), F32),
            pltpu.SemaphoreType.DMA((5,)),
        ],
        compiler_params=params(60),
        name="gate",
    )(q, k, v, z, f.T)


def beside(x):
    return jnp.concatenate([x[0], x[1]], axis=-1)


def conv_kernel(in_ref, out_ref, filt_ref, toep_ref, pad_ref, flip_ref, acc_ref, outer_ref, pos_ref, neg_ref):
    width = 2 * ROWS + 1
    nb = in_ref.shape[0] // width
    half = nb // 2
    rows = half * ROWS
    row = lax.broadcasted_iota(jnp.int32, (B, B), 0)
    lane = lax.broadcasted_iota(jnp.int32, (B, B), 1)
    filt_ref[...] = in_ref[pl.ds(2 * ROWS, nb, stride=width), :]
    toep_ref[nb * B : (nb + 1) * B, :] = jnp.zeros((B, B), BF16)

    def build(dist, before):
        taps = jnp.broadcast_to(filt_ref[pl.ds(dist, 1), :], (B, B))
        now = pltpu.roll(taps, 0, 1, stride=1, stride_axis=0)
        at = pl.multiple_of((nb - 1 - dist) * B, B)
        toep_ref[pl.ds(at, B), :] = jnp.where(lane >= row, now, before).astype(BF16)
        return now

    lax.fori_loop(0, nb, build, jnp.zeros((B, B), F32), unroll=4)

    for r in range(ROWS):
        for p in range(2):
            take = in_ref[pl.ds(r + p * width, half, stride=2 * width), :]
            pad_ref[p, pl.ds(rows + r, half, stride=ROWS), :] = take
            take = in_ref[pl.ds(ROWS + r + p * width, half, stride=2 * width), :]
            acc_ref[p, pl.ds(r, half, stride=ROWS), :] = take
    pad_ref[:, 0:rows, :] = jnp.zeros((2, rows, B), F32)
    flip = jnp.where(lane + row == B - 1, 1.0, 0.0).astype(BF16)
    flip_ref[:, 0:rows, :] = jnp.zeros((2, rows, B), F32)
    for p in range(2):
        part = pad_ref[p, rows : 2 * rows, :].astype(BF16)
        flip_ref[p, rows : 2 * rows, :] = jnp.dot(part, flip, preferred_element_type=F32)
    back_t = beside(acc_ref[...]).T.astype(BF16)
    acc_ref[...] = jnp.zeros((2, rows, B), F32)

    def step(d, carried):
        start = pl.multiple_of(rows - ROWS * d, ROWS)
        shifted = beside(pad_ref[:, pl.ds(start, rows), :]).astype(BF16)
        even = pl.multiple_of((nb - 1 - 2 * d) * B, B)
        odd = pl.multiple_of((nb - 2 - 2 * d) * B, B)
        taps = jnp.concatenate([toep_ref[pl.ds(even, 2 * B), :], toep_ref[pl.ds(odd, 2 * B), :]], axis=1)
        ahead = jnp.dot(shifted, taps, preferred_element_type=F32)
        acc_ref[0] += ahead[:, 0:B]
        acc_ref[1] += ahead[:, B : 2 * B]
        flipped = beside(flip_ref[:, pl.ds(start, rows), :]).astype(BF16)
        outer = jnp.dot(back_t, flipped, preferred_element_type=F32)
        outer_ref[2 * d] = carried + outer[0:B, B : 2 * B]
        outer_ref[2 * d + 1] = outer[0:B, 0:B] + outer[B : 2 * B, B : 2 * B]
        return outer[B : 2 * B, 0:B]

    outer_ref[nb] = lax.fori_loop(0, half, step, jnp.zeros((B, B), F32), unroll=2)

    later = (lane < row) | (lane == B - 1)

    def diagonals(dist, _):
        rolled = pltpu.roll(outer_ref[dist + 1], 0, 1, stride=1, stride_axis=0)
        kept = jnp.where(later, rolled, 0.0)
        pos_ref[pl.ds(dist, 1), :] = jnp.sum(kept, axis=0, keepdims=True)
        neg_ref[pl.ds(dist, 1), :] = jnp.sum(rolled - kept, axis=0, keepdims=True)
        return 0

    lax.fori_loop(0, nb, diagonals, 0, unroll=4)
    neg_ref[nb : nb + 1, :] = jnp.zeros((1, B), F32)
    turned = pos_ref[...] + neg_ref[1 : nb + 1, :]
    pos_ref[...] = pltpu.roll(turned, 1, 1)
    for r in range(ROWS):
        for p in range(2):
            at = pl.ds(r + p * (ROWS + 1), half, stride=2 * (ROWS + 1))
            out_ref[at, :] = acc_ref[p, pl.ds(r, half, stride=ROWS), :]
    out_ref[pl.ds(ROWS, nb, stride=ROWS + 1), :] = pos_ref[...]


def convolve(x):
    nb = x.shape[0] // (2 * ROWS + 1)
    half = nb // 2
    return pl.pallas_call(
        conv_kernel,
        out_shape=jax.ShapeDtypeStruct((nb * (ROWS + 1), B), F32),
        in_specs=[VMEM],
        out_specs=VMEM,
        scratch_shapes=[
            pltpu.VMEM((nb, B), F32),
            pltpu.VMEM(((nb + 1) * B, B), BF16),
            pltpu.VMEM((2, 2 * half * ROWS, B), F32),
            pltpu.VMEM((2, 2 * half * ROWS, B), F32),
            pltpu.VMEM((2, half * ROWS, B), F32),
            pltpu.VMEM((nb + 1, B, B), F32),
            pltpu.VMEM((nb, B), F32),
            pltpu.VMEM((nb + 8, B), F32),
        ],
        compiler_params=params(16),
        name="conv",
    )(x)


def fetch(core_ref, w_hbm, w_ref, sem):
    pairs, _, wide_n = w_ref.shape

    def copy(i):
        at = pl.multiple_of((2 * i + core_ref[0]) * wide_n, wide_n)
        return pltpu.make_async_copy(w_hbm.at[:, pl.ds(at, wide_n)], w_ref.at[i], sem.at[i])

    for i in range(pairs):
        copy(i).start()
    return lambda i: copy(i).wait()


def multiply(mixed_ref, w_ref, out_ref, wait):
    def block(i, _):
        wait(i)
        out_ref[i] = jnp.dot(mixed_ref[...], w_ref[i], preferred_element_type=F32)
        return 0

    lax.fori_loop(0, w_ref.shape[0], block, 0)


def first_kernel(core_ref, q_hbm, c_ref, w_hbm, out_ref, mixed_ref, df_ref, q_ref, turn_ref, w_ref, q_sem, w_sem):
    width = ROWS + 1
    n = c_ref.shape[0] // width
    nfilt = df_ref.shape[0]
    q_copy = pltpu.make_async_copy(q_hbm, q_ref, q_sem)
    q_copy.start()
    wait = fetch(core_ref, w_hbm, w_ref, w_sem)
    for r in range(ROWS):
        turn_ref[pl.ds(r, n, stride=ROWS), :] = c_ref[pl.ds(r, n, stride=width), :]
    share = n // nfilt
    total = c_ref[pl.ds(ROWS, nfilt, stride=share * width), :]
    for r in range(1, share):
        total += c_ref[pl.ds(r * width + ROWS, nfilt, stride=share * width), :]
    df_ref[...] = total
    q_copy.wait()
    mixed_ref[...] = (q_ref[...] * turn_ref[...].T).astype(BF16)
    multiply(mixed_ref, w_ref, out_ref, wait)


def second_kernel(core_ref, mixed_ref, w_hbm, out_ref, w_ref, w_sem):
    multiply(mixed_ref, w_ref, out_ref, fetch(core_ref, w_hbm, w_ref, w_sem))


def project(q, c, w, core, n, nfilt):
    slab, chans = q.shape
    wide_n = w.shape[1] // n
    pairs = n // 2
    cost = pl.CostEstimate(flops=slab * chans * w.shape[1], bytes_accessed=w.size, transcendentals=0)
    out = jax.ShapeDtypeStruct((pairs, slab, wide_n), F32)
    mix = jax.ShapeDtypeStruct((slab, chans), BF16)
    df = jax.ShapeDtypeStruct((nfilt, B), F32)
    smem = pl.BlockSpec(memory_space=pltpu.SMEM)
    weights = [pltpu.VMEM((pairs, chans, wide_n), BF16)]
    sems = [pltpu.SemaphoreType.DMA((pairs,))]
    theirs, mixed, df = pl.pallas_call(
        first_kernel,
        out_shape=(out, mix, df),
        in_specs=[smem, HBM, VMEM, HBM],
        out_specs=(VMEM, VMEM, VMEM),
        scratch_shapes=[
            pltpu.VMEM(q.shape, F32),
            pltpu.VMEM((chans, B), F32),
            *weights,
            pltpu.SemaphoreType.DMA(()),
            *sems,
        ],
        cost_estimate=cost,
        compiler_params=params(46),
        name="theirs",
    )((1 - core).reshape(1), q, c, w)
    mine = pl.pallas_call(
        second_kernel,
        out_shape=out,
        in_specs=[smem, VMEM, HBM],
        out_specs=VMEM,
        scratch_shapes=weights + sems,
        cost_estimate=cost,
        compiler_params=params(46),
        name="mine",
    )(core.reshape(1), mixed, w)
    return theirs, mine, df


def on_device(query, keys, values, filters, w_out, grad_z):
    parts = lax.axis_size(CONTEXT)
    n = lax.axis_size(TENSOR)
    nfilt = filters.shape[1]
    core = lax.axis_index("core").astype(jnp.int32)

    def exchange(x):
        x = x.reshape(parts, 1, -1)
        return lax.all_to_all(x, CONTEXT, split_axis=0, concat_axis=0, tiled=True).reshape(-1, B)

    whole = exchange(gate(query, keys, values, filters, grad_z, parts))
    back = exchange(convolve(whole))
    theirs, mine, grad_filters = project(query, back, w_out, core, n, nfilt)
    swapped = lax.ppermute(theirs, "core", [(0, 1), (1, 0)])
    summed = mine + swapped
    pieces = lax.all_to_all(summed, ("y", "xh"), split_axis=0, concat_axis=0, tiled=True)
    return jnp.sum(pieces, axis=0), grad_filters.T


def solution(mesh):
    fine = Mesh(
        np.asarray(mesh.devices).reshape([size for _, size in FINE]),
        [name for name, _ in FINE],
    )
    both = P(CONTEXT, TENSOR)
    return jax.shard_map(
        on_device,
        mesh=fine,
        in_specs=(both, both, both, both, P(TENSOR, None), both),
        out_specs=(both, both),
        check_vma=False,
    )
```

time: 254 us -> 204 us (0.80)
  waiting for transfers between devices: 82.5 us -> 39.8 us
  blocking collectives: 105 us -> 122 us
  Pallas kernels: 27.9 us -> 19 us
  starting transfers between devices: 28.4 us -> 20.4 us
  other arithmetic: 4.93 us -> 1.4 us
    all_to_all x2 -> x1, waiting for transfers between devices: 82.5 us -> 39 us  [exchange(): lax.all_to_all(x, CONTEXT, split_axis=0, concat_axis=0, tiled=True)]
    all_to_all x1 -> x2, blocking collectives: 105 us -> 122 us  [the longest x1 88.8 us: exchange(): lax.all_to_all(x, CONTEXT, split_axis=0, concat_axis=0, tiled=True)]
    all_to_all x2 -> x1, starting transfers between devices: 23.3 us -> 13.3 us  [exchange(): lax.all_to_all(x, CONTEXT, split_axis=0, concat_axis=0, tiled=True)]
    pallas_call x4, Pallas kernels: 27.9 us -> 19 us  [the longest x1 10.3 us: convolve(): pl.pallas_call(conv_kernel, out_shape=jax.ShapeDtypeStruct((nb * (ROWS +...]
    add x1, other arithmetic: 3.37 us -> 0.49 us  [on_device(): summed = mine + swapped]
  transfers between devices with their start and end apart: 3 -> 2, of which waited for: 2 -> 2; matrix products, arithmetic and copies ran while one was open for 1% -> 0% of each run, Pallas kernels for 3% -> 1%
where the time goes in v2:
time: 204 us
  blocking collectives  122 us (60%)
  waiting for transfers between devices  39.8 us (20%)
  starting transfers between devices  20.4 us (10%)
  Pallas kernels  19 us (9%)
    all_to_all x1, blocking collectives, exchange(): lax.all_to_all(x, CONTEXT, split_axis=0, concat_axis=0, tiled=True)  88.8 us
    all_to_all x1, waiting for transfers between devices, exchange(): lax.all_to_all(x, CONTEXT, split_axis=0, concat_axis=0, tiled=True)  39 us
    all_to_all x1, blocking collectives, on_device(): lax.all_to_all(summed, ('y', 'xh'), split_axis=0, concat_axis=0, tiled=True)  33.7 us
    all_to_all x1, starting transfers between devices, exchange(): lax.all_to_all(x, CONTEXT, split_axis=0, concat_axis=0, tiled=True)  13.3 us
    pallas_call x1, Pallas kernels, convolve(): pl.pallas_call(conv_kernel, out_shape=jax.ShapeDtypeStruct((nb * (ROWS +...  10.3 us
    ppermute x1, starting transfers between devices, on_device(): swapped = lax.ppermute(theirs, 'core', [(0, 1), (1, 0)])  7.1 us
  transfers between devices with their start and end apart: 2, of which 2 were waited for; matrix products, arithmetic and copies ran while one was open for 0% of the time, Pallas kernels for 1%

profile of v2, /device:TPU:1, one launch (start us, length us, event | category | flops | bytes accessed | tf_op | source)
XLA Modules:
  0.0 203.8 jit_solution(13442466062724496090)
XLA Ops:
  0.6 0.0 copy-start
  0.6 2.3 %gate.1 = f32[1088,128]{1,0:T(8,128)} custom-call(f32[128,512]{1,0:T(8,128)} %q_hbm.3, f32[128,512]{1,0:T(8,128)} %k_hbm.1, f32[128,512]{1,0:T(8,128)} %v_hbm.1, f32[128,512]{1,0:T(8,128)} %z_hbm.1, f32[32,128]{1,0:T(8,128)} %bitcast.11), custom_call_target="tpu_custom_call" | custom-call | tf_op jit(solution)/shard_map/gate/pallas_call | solution.py:46
  2.9 88.8 %all_to_all.15 = f32[64,1,2176]{2,1,0:T(1,128)S(1)} all-to-all(f32[64,1,2176]{2,1,0:T(1,128)} %bitcast.10), channel_id=1, replica_groups=mesh['y'=4,'xh'=2,'core'=2,'xl'=2,'z'=32] {'xl','z'}, dimensions={0} | all-to-all | bytes 1114112 | tf_op jit(solution)/shard_map/all_to_all | solution.py:252
  91.7 10.3 %conv.1 = f32[576,128]{1,0:T(8,128)} custom-call(f32[1088,128]{1,0:T(8,128)S(1)} %bitcast.8), custom_call_target="tpu_custom_call" | custom-call | tf_op jit(solution)/shard_map/conv/pallas_call | solution.py:140
  102.1 13.3 %all-to-all-start.1 = ((f32[64,1,1152]{2,1,0:T(1,128)}), f32[64,1,1152]{2,1,0:T(1,128)S(1)}, u32[]{:S(2)}, u32[]{:S(2)}) async-start(f32[64,1,1152]{2,1,0:T(1,128)} %bitcast.5), calls=%async_computation.1 | async-start | bytes 589824 | tf_op jit(solution)/shard_map/all_to_all | solution.py:252
  115.4 39.0 %all-to-all-done.1 = f32[64,1,1152]{2,1,0:T(1,128)S(1)} async-done(((f32[64,1,1152]{2,1,0:T(1,128)}), f32[64,1,1152]{2,1,0:T(1,128)S(1)}, u32[]{:S(2)}, u32[]{:S(2)}) %all-to-all-start.1) | async-done | bytes 294944 | tf_op jit(solution)/shard_map/all_to_all | solution.py:252
  154.4 0.0 copy-done
  154.4 3.4 %theirs.1 = (f32[8,128,512]{2,1,0:T(8,128)S(1)}, bf16[128,512]{1,0:T(8,128)(2,1)S(1)}, f32[32,128]{1,0:T(8,128)}) custom-call(s32[1]{0:T(128)} %bitcast.1.core_ref, f32[128,512]{1,0:T(8,128)S(1)} %copy-done, f32[576,128]{1,0:T(8,128)S(1)} %bitcast.9, bf16[512,8192]{1,0:T(8,128)(2,1)} %w_hbm.3), custom_call_target="tpu_custom_call" | custom-call | flops 536870912 | bytes 4194304 | tf_op jit(solution)/shard_map/theirs/pallas_call | solution.py:215
  157.9 7.1 %collective-permute-start = (f32[8,128,512]{2,1,0:T(8,128)S(1)}, f32[8,128,512]{2,1,0:T(8,128)S(1)}, u32[]{:S(2)}, u32[]{:S(2)}) collective-permute-start(f32[8,128,512]{2,1,0:T(8,128)S(1)} %get-tuple-element.6), channel_id=1, source_target_pairs={{0,64},{64,0},{1,65},{65,1},{2,66},{66,2},{3,67},{67,3},{4,68},{68... | collective-permute-start | bytes 6291464 | tf_op jit(solution)/shard_map/ppermute | solution.py:257
  165.0 3.0 %mine.1 = f32[8,128,512]{2,1,0:T(8,128)S(1)} custom-call(s32[1]{0:T(128)} %bitcast.core_ref, bf16[128,512]{1,0:T(8,128)(2,1)S(1)} %get-tuple-element.5.mixed_ref, bf16[512,8192]{1,0:T(8,128)(2,1)} %w_hbm.3), custom_call_target="tpu_custom_call" | custom-call | flops 536870912 | bytes 4194304 | tf_op jit(solution)/shard_map/mine/pallas_call | solution.py:231
  168.0 0.8 collective-permute-done
  168.7 0.5 add.3
  169.2 33.7 %all_to_all.16 = f32[8,128,512]{2,1,0:T(8,128)S(1)} all-to-all(f32[8,128,512]{2,1,0:T(8,128)S(1)} %add.3), channel_id=1, replica_groups=mesh['y'=4,'xh'=2,'core'=2,'xl'=2,'z'=32] {'y','xh'}, dimensions={0} | all-to-all | bytes 4194304 | tf_op jit(solution)/shard_map/all_to_all | solution.py:259
  202.9 0.9 reduce_sum.9
Async XLA Ops:
  0.6 153.8 %copy-start = (f32[128,512]{1,0:T(8,128)S(1)}, f32[128,512]{1,0:T(8,128)}, u32[]{:S(2)}) copy-start(f32[128,512]{1,0:T(8,128)} %q_hbm.3) | copy-start | bytes 786436
  102.1 52.4 %all-to-all-start.1 = ((f32[64,1,1152]{2,1,0:T(1,128)}), f32[64,1,1152]{2,1,0:T(1,128)S(1)}, u32[]{:S(2)}, u32[]{:S(2)}) async-start(f32[64,1,1152]{2,1,0:T(1,128)} %bitcast.5), calls=%async_computation.1 | async-start | bytes 589824 | tf_op jit(solution)/shard_map/all_to_all | solution.py:252
  157.9 10.9 %collective-permute-start = (f32[8,128,512]{2,1,0:T(8,128)S(1)}, f32[8,128,512]{2,1,0:T(8,128)S(1)}, u32[]{:S(2)}, u32[]{:S(2)}) collective-permute-start(f32[8,128,512]{2,1,0:T(8,128)S(1)} %get-tuple-element.6), channel_id=1, source_target_pairs={{0,64},{64,0},{1,65},{65,1},{2,66},{66,2},{3,67},{67,3},{4,68},{68... | collective-permute-start | bytes 6291464 | tf_op jit(solution)/shard_map/ppermute | solution.py:257

commit v3 on v2

--- a/solution.py
+++ b/solution.py
@@ -63,25 +63,16 @@
     return jnp.concatenate([x[0], x[1]], axis=-1)
 
 
-def conv_kernel(in_ref, out_ref, filt_ref, toep_ref, pad_ref, flip_ref, acc_ref, outer_ref, pos_ref, neg_ref):
+def conv_kernel(in_ref, out_ref, filt_ref, toep_ref, pad_ref, flip_ref, back_ref, acc_ref, outer_ref, diag_ref):
     width = 2 * ROWS + 1
     nb = in_ref.shape[0] // width
     half = nb // 2
     rows = half * ROWS
     row = lax.broadcasted_iota(jnp.int32, (B, B), 0)
     lane = lax.broadcasted_iota(jnp.int32, (B, B), 1)
-    filt_ref[...] = in_ref[pl.ds(2 * ROWS, nb, stride=width), :]
-    toep_ref[nb * B : (nb + 1) * B, :] = jnp.zeros((B, B), BF16)
-
-    def build(dist, before):
-        taps = jnp.broadcast_to(filt_ref[pl.ds(dist, 1), :], (B, B))
-        now = pltpu.roll(taps, 0, 1, stride=1, stride_axis=0)
-        at = pl.multiple_of((nb - 1 - dist) * B, B)
-        toep_ref[pl.ds(at, B), :] = jnp.where(lane >= row, now, before).astype(BF16)
-        return now
-
-    lax.fori_loop(0, nb, build, jnp.zeros((B, B), F32), unroll=4)
-
+    filt_ref[0:1, :] = jnp.zeros((1, B), F32)
+    filt_ref[nb + 1 :, :] = jnp.zeros((7, B), F32)
+    filt_ref[pl.ds(1, nb), :] = in_ref[pl.ds(2 * ROWS, nb, stride=width), :]
     for r in range(ROWS):
         for p in range(2):
             take = in_ref[pl.ds(r + p * width, half, stride=2 * width), :]
@@ -94,44 +85,64 @@
     for p in range(2):
         part = pad_ref[p, rows : 2 * rows, :].astype(BF16)
         flip_ref[p, rows : 2 * rows, :] = jnp.dot(part, flip, preferred_element_type=F32)
-    back_t = beside(acc_ref[...]).T.astype(BF16)
+    back_ref[...] = beside(acc_ref[...]).T.astype(BF16)
     acc_ref[...] = jnp.zeros((2, rows, B), F32)
-
-    def step(d, carried):
-        start = pl.multiple_of(rows - ROWS * d, ROWS)
-        shifted = beside(pad_ref[:, pl.ds(start, rows), :]).astype(BF16)
-        even = pl.multiple_of((nb - 1 - 2 * d) * B, B)
-        odd = pl.multiple_of((nb - 2 - 2 * d) * B, B)
+    outer_ref[0:4] = jnp.zeros((4, B, B), F32)
+
+    toep_ref[(nb + 2) * B :, :] = jnp.zeros((B, B), BF16)
+
+    def build(dist):
+        now = jnp.broadcast_to(filt_ref[pl.ds(dist + 1, 1), :], (B, B))
+        before = jnp.broadcast_to(filt_ref[pl.ds(dist, 1), :], (B, B))
+        block = pltpu.roll(jnp.where(lane + row < B, now, before), 0, 1, stride=1, stride_axis=0)
+        at = pl.multiple_of((nb + 1 - dist) * B, B)
+        toep_ref[pl.ds(at, B), :] = block.astype(BF16)
+
+    def diagonal(at):
+        picked = jnp.where(lane + row >= B - 1, outer_ref[at], outer_ref[at + 1])
+        rolled = pltpu.roll(picked, 0, 1, stride=1, stride_axis=0)
+        diag_ref[pl.ds(at, 1), :] = jnp.sum(rolled, axis=0, keepdims=True)
+
+    def step(d, live, deep):
+        even = pl.multiple_of((nb + 1 - 2 * d) * B, B)
+        odd = pl.multiple_of((nb - 2 * d) * B, B)
         taps = jnp.concatenate([toep_ref[pl.ds(even, 2 * B), :], toep_ref[pl.ds(odd, 2 * B), :]], axis=1)
+        start = pl.multiple_of(2 * rows - live - ROWS * d, ROWS)
+        shifted = beside(pad_ref[:, pl.ds(start, live), :]).astype(BF16)
         ahead = jnp.dot(shifted, taps, preferred_element_type=F32)
-        acc_ref[0] += ahead[:, 0:B]
-        acc_ref[1] += ahead[:, B : 2 * B]
-        flipped = beside(flip_ref[:, pl.ds(start, rows), :]).astype(BF16)
-        outer = jnp.dot(back_t, flipped, preferred_element_type=F32)
-        outer_ref[2 * d] = carried + outer[0:B, B : 2 * B]
-        outer_ref[2 * d + 1] = outer[0:B, 0:B] + outer[B : 2 * B, B : 2 * B]
-        return outer[B : 2 * B, 0:B]
-
-    outer_ref[nb] = lax.fori_loop(0, half, step, jnp.zeros((B, B), F32), unroll=2)
-
-    later = (lane < row) | (lane == B - 1)
-
-    def diagonals(dist, _):
-        rolled = pltpu.roll(outer_ref[dist + 1], 0, 1, stride=1, stride_axis=0)
-        kept = jnp.where(later, rolled, 0.0)
-        pos_ref[pl.ds(dist, 1), :] = jnp.sum(kept, axis=0, keepdims=True)
-        neg_ref[pl.ds(dist, 1), :] = jnp.sum(rolled - kept, axis=0, keepdims=True)
-        return 0
-
-    lax.fori_loop(0, nb, diagonals, 0, unroll=4)
-    neg_ref[nb : nb + 1, :] = jnp.zeros((1, B), F32)
-    turned = pos_ref[...] + neg_ref[1 : nb + 1, :]
-    pos_ref[...] = pltpu.roll(turned, 1, 1)
+        start = pl.multiple_of(2 * rows - deep - ROWS * d, ROWS)
+        flipped = beside(flip_ref[:, pl.ds(start, deep), :]).astype(BF16)
+        outer = jnp.dot(back_ref[:, rows - deep :], flipped, preferred_element_type=F32)
+        build(2 * d + 2)
+        build(2 * d + 3)
+        diagonal(2 * d)
+        diagonal(2 * d + 1)
+        acc_ref[0, rows - live :, :] += ahead[:, 0:B]
+        acc_ref[1, rows - live :, :] += ahead[:, B : 2 * B]
+        outer_ref[2 * d + 3] += outer[0:B, B : 2 * B]
+        outer_ref[2 * d + 4] = outer[0:B, 0:B] + outer[B : 2 * B, B : 2 * B]
+        outer_ref[2 * d + 5] = outer[B : 2 * B, 0:B]
+
+    build(0)
+    build(1)
+    phases = 4
+    for phase in range(phases):
+        live = rows * (phases - phase) // phases
+        deep = min(rows, -(-live // B) * B)
+
+        def some(d, _, live=live, deep=deep):
+            step(d, live, deep)
+            return 0
+
+        lax.fori_loop(half * phase // phases, half * (phase + 1) // phases, some, 0, unroll=8)
+    outer_ref[nb + 4] = jnp.zeros((B, B), F32)
+    for at in range(nb, nb + 4):
+        diagonal(at)
     for r in range(ROWS):
         for p in range(2):
             at = pl.ds(r + p * (ROWS + 1), half, stride=2 * (ROWS + 1))
             out_ref[at, :] = acc_ref[p, pl.ds(r, half, stride=ROWS), :]
-    out_ref[pl.ds(ROWS, nb, stride=ROWS + 1), :] = pos_ref[...]
+    out_ref[pl.ds(ROWS, nb, stride=ROWS + 1), :] = pltpu.roll(diag_ref[pl.ds(4, nb), :], 1, 1)
 
 
 def convolve(x):
@@ -143,13 +154,13 @@
         in_specs=[VMEM],
         out_specs=VMEM,
         scratch_shapes=[
-            pltpu.VMEM((nb, B), F32),
-            pltpu.VMEM(((nb + 1) * B, B), BF16),
+            pltpu.VMEM((nb + 8, B), F32),
+            pltpu.VMEM(((nb + 3) * B, B), BF16),
             pltpu.VMEM((2, 2 * half * ROWS, B), F32),
             pltpu.VMEM((2, 2 * half * ROWS, B), F32),
+            pltpu.VMEM((2 * B, half * ROWS), BF16),
             pltpu.VMEM((2, half * ROWS, B), F32),
-            pltpu.VMEM((nb + 1, B, B), F32),
-            pltpu.VMEM((nb, B), F32),
+            pltpu.VMEM((nb + 6, B, B), F32),
             pltpu.VMEM((nb + 8, B), F32),
         ],
         compiler_params=params(16),

time: 204 us -> 197 us (0.966)
  Pallas kernels: 19 us -> 11.8 us
    pallas_call x1, Pallas kernels: 10.3 us -> 3.16 us  [convolve(): pl.pallas_call(conv_kernel, out_shape=jax.ShapeDtypeStruct((nb * (ROWS +...]
  transfers between devices with their start and end apart: 2 -> 2, of which waited for: 2 -> 2; matrix products, arithmetic and copies ran while one was open for 0% -> 0% of each run, Pallas kernels for 1% -> 2%
where the time goes in v3:
time: 197 us
  blocking collectives  123 us (62%)
  waiting for transfers between devices  39.8 us (20%)
  starting transfers between devices  20.4 us (10%)
  Pallas kernels  11.8 us (6%)
    all_to_all x1, blocking collectives, exchange(): lax.all_to_all(x, CONTEXT, split_axis=0, concat_axis=0, tiled=True)  88.8 us
    all_to_all x1, waiting for transfers between devices, exchange(): lax.all_to_all(x, CONTEXT, split_axis=0, concat_axis=0, tiled=True)  39 us
    all_to_all x1, blocking collectives, on_device(): lax.all_to_all(summed, ('y', 'xh'), split_axis=0, concat_axis=0, tiled=True)  33.7 us
    all_to_all x1, starting transfers between devices, exchange(): lax.all_to_all(x, CONTEXT, split_axis=0, concat_axis=0, tiled=True)  13.3 us
    ppermute x1, starting transfers between devices, on_device(): swapped = lax.ppermute(theirs, 'core', [(0, 1), (1, 0)])  7.09 us
  transfers between devices with their start and end apart: 2, of which 2 were waited for; matrix products, arithmetic and copies ran while one was open for 0% of the time, Pallas kernels for 2%

profile of v3, /device:TPU:1, one launch (start us, length us, event | category | flops | bytes accessed | tf_op | source)
XLA Modules:
  0.0 196.7 jit_solution(7190602934507857095)
XLA Ops:
  0.6 0.0 copy-start
  0.6 2.3 %gate.1 = f32[1088,128]{1,0:T(8,128)} custom-call(f32[128,512]{1,0:T(8,128)} %q_hbm.3, f32[128,512]{1,0:T(8,128)} %k_hbm.1, f32[128,512]{1,0:T(8,128)} %v_hbm.1, f32[128,512]{1,0:T(8,128)} %z_hbm.1, f32[32,128]{1,0:T(8,128)} %bitcast.11), custom_call_target="tpu_custom_call" | custom-call | tf_op jit(solution)/shard_map/gate/pallas_call | solution.py:46
  2.9 88.8 %all_to_all.15 = f32[64,1,2176]{2,1,0:T(1,128)S(1)} all-to-all(f32[64,1,2176]{2,1,0:T(1,128)} %bitcast.10), channel_id=1, replica_groups=mesh['y'=4,'xh'=2,'core'=2,'xl'=2,'z'=32] {'xl','z'}, dimensions={0} | all-to-all | bytes 1114112 | tf_op jit(solution)/shard_map/all_to_all | solution.py:263
  91.7 3.2 %conv.1 = f32[576,128]{1,0:T(8,128)} custom-call(f32[1088,128]{1,0:T(8,128)S(1)} %bitcast.8), custom_call_target="tpu_custom_call" | custom-call | tf_op jit(solution)/shard_map/conv/pallas_call | solution.py:151
  94.9 13.3 %all-to-all-start.1 = ((f32[64,1,1152]{2,1,0:T(1,128)}), f32[64,1,1152]{2,1,0:T(1,128)S(1)}, u32[]{:S(2)}, u32[]{:S(2)}) async-start(f32[64,1,1152]{2,1,0:T(1,128)} %bitcast.5), calls=%async_computation.1 | async-start | bytes 589824 | tf_op jit(solution)/shard_map/all_to_all | solution.py:263
  108.2 39.0 %all-to-all-done.1 = f32[64,1,1152]{2,1,0:T(1,128)S(1)} async-done(((f32[64,1,1152]{2,1,0:T(1,128)}), f32[64,1,1152]{2,1,0:T(1,128)S(1)}, u32[]{:S(2)}, u32[]{:S(2)}) %all-to-all-start.1) | async-done | bytes 294944 | tf_op jit(solution)/shard_map/all_to_all | solution.py:263
  147.3 0.0 copy-done
  147.3 3.4 %theirs.1 = (f32[8,128,512]{2,1,0:T(8,128)S(1)}, bf16[128,512]{1,0:T(8,128)(2,1)S(1)}, f32[32,128]{1,0:T(8,128)}) custom-call(s32[1]{0:T(128)} %bitcast.1.core_ref, f32[128,512]{1,0:T(8,128)S(1)} %copy-done, f32[576,128]{1,0:T(8,128)S(1)} %bitcast.9, bf16[512,8192]{1,0:T(8,128)(2,1)} %w_hbm.3), custom_call_target="tpu_custom_call" | custom-call | flops 536870912 | bytes 4194304 | tf_op jit(solution)/shard_map/theirs/pallas_call | solution.py:226
  150.7 7.1 %collective-permute-start = (f32[8,128,512]{2,1,0:T(8,128)S(1)}, f32[8,128,512]{2,1,0:T(8,128)S(1)}, u32[]{:S(2)}, u32[]{:S(2)}) collective-permute-start(f32[8,128,512]{2,1,0:T(8,128)S(1)} %get-tuple-element.6), channel_id=1, source_target_pairs={{0,64},{64,0},{1,65},{65,1},{2,66},{66,2},{3,67},{67,3},{4,68},{68... | collective-permute-start | bytes 6291464 | tf_op jit(solution)/shard_map/ppermute | solution.py:268
  157.8 3.0 %mine.1 = f32[8,128,512]{2,1,0:T(8,128)S(1)} custom-call(s32[1]{0:T(128)} %bitcast.core_ref, bf16[128,512]{1,0:T(8,128)(2,1)S(1)} %get-tuple-element.5.mixed_ref, bf16[512,8192]{1,0:T(8,128)(2,1)} %w_hbm.3), custom_call_target="tpu_custom_call" | custom-call | flops 536870912 | bytes 4194304 | tf_op jit(solution)/shard_map/mine/pallas_call | solution.py:242
  160.8 0.8 collective-permute-done
  161.6 0.5 add.3
  162.0 33.7 %all_to_all.16 = f32[8,128,512]{2,1,0:T(8,128)S(1)} all-to-all(f32[8,128,512]{2,1,0:T(8,128)S(1)} %add.3), channel_id=1, replica_groups=mesh['y'=4,'xh'=2,'core'=2,'xl'=2,'z'=32] {'y','xh'}, dimensions={0} | all-to-all | bytes 4194304 | tf_op jit(solution)/shard_map/all_to_all | solution.py:270
  195.8 0.9 reduce_sum.9
Async XLA Ops:
  0.6 146.6 %copy-start = (f32[128,512]{1,0:T(8,128)S(1)}, f32[128,512]{1,0:T(8,128)}, u32[]{:S(2)}) copy-start(f32[128,512]{1,0:T(8,128)} %q_hbm.3) | copy-start | bytes 786436
  94.9 52.4 %all-to-all-start.1 = ((f32[64,1,1152]{2,1,0:T(1,128)}), f32[64,1,1152]{2,1,0:T(1,128)S(1)}, u32[]{:S(2)}, u32[]{:S(2)}) async-start(f32[64,1,1152]{2,1,0:T(1,128)} %bitcast.5), calls=%async_computation.1 | async-start | bytes 589824 | tf_op jit(solution)/shard_map/all_to_all | solution.py:263
  150.7 10.9 %collective-permute-start = (f32[8,128,512]{2,1,0:T(8,128)S(1)}, f32[8,128,512]{2,1,0:T(8,128)S(1)}, u32[]{:S(2)}, u32[]{:S(2)}) collective-permute-start(f32[8,128,512]{2,1,0:T(8,128)S(1)} %get-tuple-element.6), channel_id=1, source_target_pairs={{0,64},{64,0},{1,65},{65,1},{2,66},{66,2},{3,67},{67,3},{4,68},{68... | collective-permute-start | bytes 6291464 | tf_op jit(solution)/shard_map/ppermute | solution.py:268

commit v4 on v3

--- a/solution.py
+++ b/solution.py
@@ -21,25 +21,44 @@
     return pltpu.CompilerParams(vmem_limit_bytes=mib << 20)
 
 
-def gate_kernel(q_hbm, k_hbm, v_hbm, z_hbm, f_hbm, out_ref, in_ref, f_ref, turn_ref, sem):
+def gate_kernel(q_hbm, k_hbm, v_hbm, z_hbm, f_hbm, out_hbm, in_ref, f_ref, turn_ref, out_ref, sem, f_sem, out_sem):
     width = 2 * ROWS + 1
-    n = out_ref.shape[0] // width
-    share = n // f_ref.shape[0]
-    copies = [pltpu.make_async_copy(f_hbm, f_ref, sem.at[4])]
-    for i, hbm in enumerate((k_hbm, v_hbm, z_hbm, q_hbm)):
-        copies.append(pltpu.make_async_copy(hbm, in_ref.at[i], sem.at[i]))
-    for copy in copies:
-        copy.start()
-    copies[0].wait()
+    groups = out_sem.shape[0]
+    n = out_ref.shape[0] // width // groups
+    share = n * groups // f_ref.shape[0]
+    pairs = ((k_hbm, v_hbm), (z_hbm, q_hbm))
+
+    def fetch(g, i, j):
+        at = pl.ds(g * B, B)
+        return pltpu.make_async_copy(pairs[i][j].at[:, at], in_ref.at[2 * i + j, :, at], sem.at[g, 2 * i + j])
+
+    def send(g):
+        at = pl.ds(g * n * width, n * width)
+        return pltpu.make_async_copy(out_ref.at[at], out_hbm.at[at], out_sem.at[g])
+
+    f_copy = pltpu.make_async_copy(f_hbm, f_ref, f_sem)
+    for g in range(groups):
+        for i in range(2):
+            for j in range(2):
+                fetch(g, i, j).start()
+        if g == 0:
+            f_copy.start()
+    f_copy.wait()
     for r in range(share):
-        out_ref[pl.ds(r * width + 2 * ROWS, n // share, stride=share * width), :] = f_ref[...]
-    for i in range(2):
-        copies[2 * i + 1].wait()
-        copies[2 * i + 2].wait()
-        turn_ref[i] = (in_ref[2 * i] * in_ref[2 * i + 1]).T
-        for r in range(ROWS):
-            rows = turn_ref[i, pl.ds(r, n, stride=ROWS), :]
-            out_ref[pl.ds(i * ROWS + r, n, stride=width), :] = rows
+        at = pl.ds(r * width + 2 * ROWS, f_ref.shape[0], stride=share * width)
+        out_ref[at, :] = f_ref[...]
+    for g in range(groups):
+        for i in range(2):
+            fetch(g, i, 0).wait()
+            fetch(g, i, 1).wait()
+            at = pl.ds(g * B, B)
+            turn_ref[i, at, :] = (in_ref[2 * i, :, at] * in_ref[2 * i + 1, :, at]).T
+            for r in range(ROWS):
+                rows = turn_ref[i, pl.ds(g * B + r, n, stride=ROWS), :]
+                out_ref[pl.ds(g * n * width + i * ROWS + r, n, stride=width), :] = rows
+        send(g).start()
+    for g in range(groups):
+        send(g).wait()
 
 
 def gate(q, k, v, f, z, parts):
@@ -47,12 +66,15 @@
         gate_kernel,
         out_shape=jax.ShapeDtypeStruct((parts * (2 * ROWS + 1), B), F32),
         in_specs=[HBM] * 5,
-        out_specs=VMEM,
+        out_specs=HBM,
         scratch_shapes=[
             pltpu.VMEM((4,) + q.shape, F32),
             pltpu.VMEM(f.shape[::-1], F32),
             pltpu.VMEM((2, q.shape[1], B), F32),
-            pltpu.SemaphoreType.DMA((5,)),
+            pltpu.VMEM((parts * (2 * ROWS + 1), B), F32),
+            pltpu.SemaphoreType.DMA((q.shape[1] // B, 4)),
+            pltpu.SemaphoreType.DMA(()),
+            pltpu.SemaphoreType.DMA((q.shape[1] // B,)),
         ],
         compiler_params=params(60),
         name="gate",
@@ -168,83 +190,103 @@
     )(x)
 
 
-def fetch(core_ref, w_hbm, w_ref, sem):
-    pairs, _, wide_n = w_ref.shape
+def fetch(core_ref, w_hbm, w_ref, sem, first):
+    blocks, _, wide_n = w_ref.shape
 
     def copy(i):
-        at = pl.multiple_of((2 * i + core_ref[0]) * wide_n, wide_n)
+        at = pl.multiple_of((2 * (first + i) + core_ref[0]) * wide_n, wide_n)
         return pltpu.make_async_copy(w_hbm.at[:, pl.ds(at, wide_n)], w_ref.at[i], sem.at[i])
 
-    for i in range(pairs):
+    for i in range(blocks):
         copy(i).start()
     return lambda i: copy(i).wait()
 
 
-def multiply(mixed_ref, w_ref, out_ref, wait):
-    def block(i, _):
+def fetch_kernel(core_ref, after_ref, w_hbm, out_ref, sem):
+    wait = fetch(core_ref, w_hbm, out_ref, sem, 0)
+    for i in range(out_ref.shape[0]):
         wait(i)
-        out_ref[i] = jnp.dot(mixed_ref[...], w_ref[i], preferred_element_type=F32)
-        return 0
-
-    lax.fori_loop(0, w_ref.shape[0], block, 0)
-
-
-def first_kernel(core_ref, q_hbm, c_ref, w_hbm, out_ref, mixed_ref, df_ref, q_ref, turn_ref, w_ref, q_sem, w_sem):
+
+
+def multiply(mixed_ref, w_ref, out_ref, first):
+    for i in range(w_ref.shape[0]):
+        out_ref[first + i] = jnp.dot(mixed_ref[...], w_ref[i], preferred_element_type=F32)
+
+
+def first_kernel(core_ref, q_ref, c_ref, ahead_ref, w_hbm, out_ref, mixed_ref, df_ref, turn_ref, w_ref, w_sem):
     width = ROWS + 1
     n = c_ref.shape[0] // width
     nfilt = df_ref.shape[0]
-    q_copy = pltpu.make_async_copy(q_hbm, q_ref, q_sem)
-    q_copy.start()
-    wait = fetch(core_ref, w_hbm, w_ref, w_sem)
+    early = ahead_ref.shape[0]
+    wait = fetch(core_ref, w_hbm, w_ref, w_sem, early)
     for r in range(ROWS):
         turn_ref[pl.ds(r, n, stride=ROWS), :] = c_ref[pl.ds(r, n, stride=width), :]
+    mixed_ref[...] = (q_ref[...] * turn_ref[...].T).astype(BF16)
     share = n // nfilt
     total = c_ref[pl.ds(ROWS, nfilt, stride=share * width), :]
     for r in range(1, share):
         total += c_ref[pl.ds(r * width + ROWS, nfilt, stride=share * width), :]
     df_ref[...] = total
-    q_copy.wait()
-    mixed_ref[...] = (q_ref[...] * turn_ref[...].T).astype(BF16)
-    multiply(mixed_ref, w_ref, out_ref, wait)
+    multiply(mixed_ref, ahead_ref, out_ref, 0)
+    for i in range(w_ref.shape[0]):
+        wait(i)
+    multiply(mixed_ref, w_ref, out_ref, early)
 
 
 def second_kernel(core_ref, mixed_ref, w_hbm, out_ref, w_ref, w_sem):
-    multiply(mixed_ref, w_ref, out_ref, fetch(core_ref, w_hbm, w_ref, w_sem))
-
-
-def project(q, c, w, core, n, nfilt):
+    wait = fetch(core_ref, w_hbm, w_ref, w_sem, 0)
+    half = w_ref.shape[0] // 2
+    for start in (0, half):
+        for i in range(half):
+            wait(start + i)
+        multiply(mixed_ref, w_ref.at[start : start + half], out_ref, start)
+
+
+SMEM = pl.BlockSpec(memory_space=pltpu.SMEM)
+
+
+def prefetch(after, w, core, n):
+    shape = (n // 4, w.shape[0], w.shape[1] // n)
+    return pl.pallas_call(
+        fetch_kernel,
+        out_shape=jax.ShapeDtypeStruct(shape, BF16),
+        in_specs=[SMEM, pl.BlockSpec(memory_space=pl.ANY), HBM],
+        out_specs=VMEM,
+        scratch_shapes=[pltpu.SemaphoreType.DMA(shape[:1])],
+        cost_estimate=pl.CostEstimate(flops=0, bytes_accessed=w.size, transcendentals=0),
+        compiler_params=params(46),
+        name="prefetch",
+    )((1 - core).reshape(1), after, w)
+
+
+def project(q, c, w, w_theirs, core, nfilt):
     slab, chans = q.shape
-    wide_n = w.shape[1] // n
-    pairs = n // 2
+    early, _, wide_n = w_theirs.shape
+    pairs = w.shape[1] // wide_n // 2
     cost = pl.CostEstimate(flops=slab * chans * w.shape[1], bytes_accessed=w.size, transcendentals=0)
     out = jax.ShapeDtypeStruct((pairs, slab, wide_n), F32)
     mix = jax.ShapeDtypeStruct((slab, chans), BF16)
     df = jax.ShapeDtypeStruct((nfilt, B), F32)
-    smem = pl.BlockSpec(memory_space=pltpu.SMEM)
-    weights = [pltpu.VMEM((pairs, chans, wide_n), BF16)]
-    sems = [pltpu.SemaphoreType.DMA((pairs,))]
     theirs, mixed, df = pl.pallas_call(
         first_kernel,
         out_shape=(out, mix, df),
-        in_specs=[smem, HBM, VMEM, HBM],
+        in_specs=[SMEM, VMEM, VMEM, VMEM, HBM],
         out_specs=(VMEM, VMEM, VMEM),
         scratch_shapes=[
-            pltpu.VMEM(q.shape, F32),
             pltpu.VMEM((chans, B), F32),
-            *weights,
-            pltpu.SemaphoreType.DMA(()),
-            *sems,
+            pltpu.VMEM((pairs - early, chans, wide_n), BF16),
+            pltpu.SemaphoreType.DMA((pairs - early,)),
         ],
         cost_estimate=cost,
         compiler_params=params(46),
         name="theirs",
-    )((1 - core).reshape(1), q, c, w)
+    )((1 - core).reshape(1), q, c, w_theirs, w)
     mine = pl.pallas_call(
         second_kernel,
         out_shape=out,
-        in_specs=[smem, VMEM, HBM],
+        in_specs=[SMEM, VMEM, HBM],
         out_specs=VMEM,
-        scratch_shapes=weights + sems,
+        scratch_shapes=[pltpu.VMEM((pairs, chans, wide_n), BF16), pltpu.SemaphoreType.DMA((pairs,))],
         cost_estimate=cost,
         compiler_params=params(46),
         name="mine",
@@ -263,8 +305,10 @@
         return lax.all_to_all(x, CONTEXT, split_axis=0, concat_axis=0, tiled=True).reshape(-1, B)
 
     whole = exchange(gate(query, keys, values, filters, grad_z, parts))
-    back = exchange(convolve(whole))
-    theirs, mine, grad_filters = project(query, back, w_out, core, n, nfilt)
+    result = convolve(whole)
+    w_theirs = prefetch(result, w_out, core, n)
+    back = exchange(result)
+    theirs, mine, grad_filters = project(query, back, w_out, w_theirs, core, nfilt)
     swapped = lax.ppermute(theirs, "core", [(0, 1), (1, 0)])
     summed = mine + swapped
     pieces = lax.all_to_all(summed, ("y", "xh"), split_axis=0, concat_axis=0, tiled=True)

time: 197 us -> 197 us (level)
    pallas_call x2 -> x3, Pallas kernels: 6.43 us -> 6.83 us  [the longest x1 2.7 us: project(): pl.pallas_call(second_kernel, out_shape=out, in_specs=[SMEM, VMEM, HBM],...]
where the time goes in v4:
time: 197 us; the launch traced here: 196 us
  blocking collectives  123 us (62%)
  waiting for transfers between devices  38.4 us (19%)
  starting transfers between devices  20.4 us (10%)
  Pallas kernels  12.9 us (7%)
    all_to_all x1, blocking collectives, exchange(): lax.all_to_all(x, CONTEXT, split_axis=0, concat_axis=0, tiled=True)  88.8 us
    all_to_all x1, waiting for transfers between devices, exchange(): lax.all_to_all(x, CONTEXT, split_axis=0, concat_axis=0, tiled=True)  37.4 us
    all_to_all x1, blocking collectives, on_device(): lax.all_to_all(summed, ('y', 'xh'), split_axis=0, concat_axis=0, tiled=True)  33.7 us
    all_to_all x1, starting transfers between devices, exchange(): lax.all_to_all(x, CONTEXT, split_axis=0, concat_axis=0, tiled=True)  13.3 us
    ppermute x1, starting transfers between devices, on_device(): swapped = lax.ppermute(theirs, 'core', [(0, 1), (1, 0)])  7.1 us
  transfers between devices with their start and end apart: 2, of which 2 were waited for; matrix products, arithmetic and copies ran while one was open for 0% of the time, Pallas kernels for 2%

profile of v4, /device:TPU:1, one launch (start us, length us, event | category | flops | bytes accessed | tf_op | source)
XLA Modules:
  0.0 196.4 jit_solution(14836598553405116941)
XLA Ops:
  0.6 2.9 %gate.1 = f32[1088,128]{1,0:T(8,128)} custom-call(f32[128,512]{1,0:T(8,128)} %q_ref.1, f32[128,512]{1,0:T(8,128)} %k_hbm.1, f32[128,512]{1,0:T(8,128)} %v_hbm.1, f32[128,512]{1,0:T(8,128)} %z_hbm.1, f32[32,128]{1,0:T(8,128)} %bitcast.11), custom_call_target="tpu_custom_call" | custom-call | tf_op jit(solution)/shard_map/gate/pallas_call | solution.py:65
  3.6 88.8 %all_to_all.15 = f32[64,1,2176]{2,1,0:T(1,128)S(1)} all-to-all(f32[64,1,2176]{2,1,0:T(1,128)} %bitcast.10), channel_id=1, replica_groups=mesh['y'=4,'xh'=2,'core'=2,'xl'=2,'z'=32] {'xl','z'}, dimensions={0} | all-to-all | bytes 1114112 | tf_op jit(solution)/shard_map/all_to_all | solution.py:305
  92.4 3.2 %conv.1.after_ref = f32[576,128]{1,0:T(8,128)} custom-call(f32[1088,128]{1,0:T(8,128)S(1)} %bitcast.8), custom_call_target="tpu_custom_call" | custom-call | tf_op jit(solution)/shard_map/conv/pallas_call | solution.py:173
  95.5 13.3 %all-to-all-start.1 = ((f32[64,1,1152]{2,1,0:T(1,128)}), f32[64,1,1152]{2,1,0:T(1,128)S(1)}, u32[]{:S(2)}, u32[]{:S(2)}) async-start(f32[64,1,1152]{2,1,0:T(1,128)} %bitcast.5), calls=%async_computation.1 | async-start | bytes 589824 | tf_op jit(solution)/shard_map/all_to_all | solution.py:305
  108.9 0.0 copy-start
  108.9 1.6 prefetch.1.ahead_ref
  110.5 37.4 %all-to-all-done.1 = f32[64,1,1152]{2,1,0:T(1,128)S(1)} async-done(((f32[64,1,1152]{2,1,0:T(1,128)}), f32[64,1,1152]{2,1,0:T(1,128)S(1)}, u32[]{:S(2)}, u32[]{:S(2)}) %all-to-all-start.1) | async-done | bytes 294944 | tf_op jit(solution)/shard_map/all_to_all | solution.py:305
  147.9 0.0 copy-done
  147.9 2.5 %theirs.1 = (f32[8,128,512]{2,1,0:T(8,128)S(1)}, bf16[128,512]{1,0:T(8,128)(2,1)S(1)}, f32[32,128]{1,0:T(8,128)}) custom-call(s32[1]{0:T(128)} %bitcast.1.core_ref, f32[128,512]{1,0:T(8,128)S(1)} %copy-done, f32[576,128]{1,0:T(8,128)S(1)} %bitcast.9, bf16[4,512,512]{2,1,0:T(8,128)(2,1)S(1)} %prefetch.1.ahead_ref, bf16[512,8192]{1,0:T(8,128)(2,1)} %w_hbm.5), custom_call_target="tpu_custom_call" | custom-call | flops 536870912 | bytes 4194304 | tf_op jit(solution)/shard_map/theirs/pallas_call | solution.py:270
  150.4 7.1 %collective-permute-start = (f32[8,128,512]{2,1,0:T(8,128)S(1)}, f32[8,128,512]{2,1,0:T(8,128)S(1)}, u32[]{:S(2)}, u32[]{:S(2)}) collective-permute-start(f32[8,128,512]{2,1,0:T(8,128)S(1)} %get-tuple-element.6), channel_id=1, source_target_pairs={{0,64},{64,0},{1,65},{65,1},{2,66},{66,2},{3,67},{67,3},{4,68},{68... | collective-permute-start | bytes 6291464 | tf_op jit(solution)/shard_map/ppermute | solution.py:312
  157.5 2.7 %mine.1 = f32[8,128,512]{2,1,0:T(8,128)S(1)} custom-call(s32[1]{0:T(128)} %bitcast.core_ref, bf16[128,512]{1,0:T(8,128)(2,1)S(1)} %get-tuple-element.5.mixed_ref, bf16[512,8192]{1,0:T(8,128)(2,1)} %w_hbm.5), custom_call_target="tpu_custom_call" | custom-call | flops 536870912 | bytes 4194304 | tf_op jit(solution)/shard_map/mine/pallas_call | solution.py:284
  160.2 1.1 collective-permute-done
  161.3 0.5 add.3
  161.8 33.7 %all_to_all.16 = f32[8,128,512]{2,1,0:T(8,128)S(1)} all-to-all(f32[8,128,512]{2,1,0:T(8,128)S(1)} %add.3), channel_id=1, replica_groups=mesh['y'=4,'xh'=2,'core'=2,'xl'=2,'z'=32] {'y','xh'}, dimensions={0} | all-to-all | bytes 4194304 | tf_op jit(solution)/shard_map/all_to_all | solution.py:314
  195.5 0.9 reduce_sum.9
Async XLA Ops:
  95.5 52.4 %all-to-all-start.1 = ((f32[64,1,1152]{2,1,0:T(1,128)}), f32[64,1,1152]{2,1,0:T(1,128)S(1)}, u32[]{:S(2)}, u32[]{:S(2)}) async-start(f32[64,1,1152]{2,1,0:T(1,128)} %bitcast.5), calls=%async_computation.1 | async-start | bytes 589824 | tf_op jit(solution)/shard_map/all_to_all | solution.py:305
  108.9 39.0 %copy-start = (f32[128,512]{1,0:T(8,128)S(1)}, f32[128,512]{1,0:T(8,128)}, u32[]{:S(2)}) copy-start(f32[128,512]{1,0:T(8,128)} %q_ref.1) | copy-start | bytes 786436
  150.4 10.9 %collective-permute-start = (f32[8,128,512]{2,1,0:T(8,128)S(1)}, f32[8,128,512]{2,1,0:T(8,128)S(1)}, u32[]{:S(2)}, u32[]{:S(2)}) collective-permute-start(f32[8,128,512]{2,1,0:T(8,128)S(1)} %get-tuple-element.6), channel_id=1, source_target_pairs={{0,64},{64,0},{1,65},{65,1},{2,66},{66,2},{3,67},{67,3},{4,68},{68... | collective-permute-start | bytes 6291464 | tf_op jit(solution)/shard_map/ppermute | solution.py:312

commit v5 on v4

--- a/solution.py
+++ b/solution.py
@@ -15,70 +15,54 @@
 BF16 = jnp.bfloat16
 VMEM = pl.BlockSpec(memory_space=pltpu.VMEM)
 HBM = pl.BlockSpec(memory_space=pltpu.HBM)
+SMEM = pl.BlockSpec(memory_space=pltpu.SMEM)
+LATER_NS = 12000
 
 
 def params(mib):
     return pltpu.CompilerParams(vmem_limit_bytes=mib << 20)
 
 
-def gate_kernel(q_hbm, k_hbm, v_hbm, z_hbm, f_hbm, out_hbm, in_ref, f_ref, turn_ref, out_ref, sem, f_sem, out_sem):
+def gate_kernel(wait_ref, q_hbm, k_hbm, v_hbm, z_hbm, f_hbm, out_ref, in_ref, f_ref, turn_ref, sem):
     width = 2 * ROWS + 1
-    groups = out_sem.shape[0]
-    n = out_ref.shape[0] // width // groups
-    share = n * groups // f_ref.shape[0]
-    pairs = ((k_hbm, v_hbm), (z_hbm, q_hbm))
-
-    def fetch(g, i, j):
-        at = pl.ds(g * B, B)
-        return pltpu.make_async_copy(pairs[i][j].at[:, at], in_ref.at[2 * i + j, :, at], sem.at[g, 2 * i + j])
-
-    def send(g):
-        at = pl.ds(g * n * width, n * width)
-        return pltpu.make_async_copy(out_ref.at[at], out_hbm.at[at], out_sem.at[g])
-
-    f_copy = pltpu.make_async_copy(f_hbm, f_ref, f_sem)
-    for g in range(groups):
-        for i in range(2):
-            for j in range(2):
-                fetch(g, i, j).start()
-        if g == 0:
-            f_copy.start()
-    f_copy.wait()
+    n = out_ref.shape[0] // width
+    share = n // f_ref.shape[0]
+    copies = [pltpu.make_async_copy(f_hbm, f_ref, sem.at[4])]
+    for i, hbm in enumerate((k_hbm, v_hbm, z_hbm, q_hbm)):
+        copies.append(pltpu.make_async_copy(hbm, in_ref.at[i], sem.at[i]))
+    for copy in copies:
+        copy.start()
+    copies[0].wait()
     for r in range(share):
-        at = pl.ds(r * width + 2 * ROWS, f_ref.shape[0], stride=share * width)
-        out_ref[at, :] = f_ref[...]
-    for g in range(groups):
-        for i in range(2):
-            fetch(g, i, 0).wait()
-            fetch(g, i, 1).wait()
-            at = pl.ds(g * B, B)
-            turn_ref[i, at, :] = (in_ref[2 * i, :, at] * in_ref[2 * i + 1, :, at]).T
-            for r in range(ROWS):
-                rows = turn_ref[i, pl.ds(g * B + r, n, stride=ROWS), :]
-                out_ref[pl.ds(g * n * width + i * ROWS + r, n, stride=width), :] = rows
-        send(g).start()
-    for g in range(groups):
-        send(g).wait()
-
-
-def gate(q, k, v, f, z, parts):
+        out_ref[pl.ds(r * width + 2 * ROWS, n // share, stride=share * width), :] = f_ref[...]
+    for i in range(2):
+        copies[2 * i + 1].wait()
+        copies[2 * i + 2].wait()
+        turn_ref[i] = (in_ref[2 * i] * in_ref[2 * i + 1]).T
+        for r in range(ROWS):
+            rows = turn_ref[i, pl.ds(r, n, stride=ROWS), :]
+            out_ref[pl.ds(i * ROWS + r, n, stride=width), :] = rows
+
+    @pl.when(wait_ref[0] == 1)
+    def _():
+        pl.delay(LATER_NS)
+
+
+def gate(q, k, v, f, z, parts, later):
     return pl.pallas_call(
         gate_kernel,
         out_shape=jax.ShapeDtypeStruct((parts * (2 * ROWS + 1), B), F32),
-        in_specs=[HBM] * 5,
-        out_specs=HBM,
+        in_specs=[SMEM] + [HBM] * 5,
+        out_specs=VMEM,
         scratch_shapes=[
             pltpu.VMEM((4,) + q.shape, F32),
             pltpu.VMEM(f.shape[::-1], F32),
             pltpu.VMEM((2, q.shape[1], B), F32),
-            pltpu.VMEM((parts * (2 * ROWS + 1), B), F32),
-            pltpu.SemaphoreType.DMA((q.shape[1] // B, 4)),
-            pltpu.SemaphoreType.DMA(()),
-            pltpu.SemaphoreType.DMA((q.shape[1] // B,)),
+            pltpu.SemaphoreType.DMA((5,)),
         ],
         compiler_params=params(60),
         name="gate",
-    )(q, k, v, z, f.T)
+    )(later.reshape(1), q, k, v, z, f.T)
 
 
 def beside(x):
@@ -240,9 +224,6 @@
         for i in range(half):
             wait(start + i)
         multiply(mixed_ref, w_ref.at[start : start + half], out_ref, start)
-
-
-SMEM = pl.BlockSpec(memory_space=pltpu.SMEM)
 
 
 def prefetch(after, w, core, n):
@@ -304,7 +285,7 @@
         x = x.reshape(parts, 1, -1)
         return lax.all_to_all(x, CONTEXT, split_axis=0, concat_axis=0, tiled=True).reshape(-1, B)
 
-    whole = exchange(gate(query, keys, values, filters, grad_z, parts))
+    whole = exchange(gate(query, keys, values, filters, grad_z, parts, 1 - core))
     result = convolve(whole)
     w_theirs = prefetch(result, w_out, core, n)
     back = exchange(result)

time: 197 us -> 188 us (0.954)
  blocking collectives: 123 us -> 110 us
  starting transfers between devices: 20.4 us -> 32.6 us
  waiting for transfers between devices: 38.4 us -> 30.8 us
    all_to_all x1, blocking collectives: 88.8 us -> 76.6 us  [exchange(): lax.all_to_all(x, CONTEXT, split_axis=0, concat_axis=0, tiled=True)]
    ppermute x1, starting transfers between devices: 7.1 us -> 14.9 us  [on_device(): swapped = lax.ppermute(theirs, 'core', [(0, 1), (1, 0)])]
    all_to_all x1, waiting for transfers between devices: 37.4 us -> 29.7 us  [exchange(): lax.all_to_all(x, CONTEXT, split_axis=0, concat_axis=0, tiled=True)]
    all_to_all x1, starting transfers between devices: 13.3 us -> 17.6 us  [exchange(): lax.all_to_all(x, CONTEXT, split_axis=0, concat_axis=0, tiled=True)]
where the time goes in v5:
time: 188 us
  blocking collectives  110 us (59%)
  starting transfers between devices  32.6 us (17%)
  waiting for transfers between devices  30.8 us (16%)
  Pallas kernels  12.2 us (6%)
    all_to_all x1, blocking collectives, exchange(): lax.all_to_all(x, CONTEXT, split_axis=0, concat_axis=0, tiled=True)  76.6 us
    all_to_all x1, blocking collectives, on_device(): lax.all_to_all(summed, ('y', 'xh'), split_axis=0, concat_axis=0, tiled=True)  33.7 us
    all_to_all x1, waiting for transfers between devices, exchange(): lax.all_to_all(x, CONTEXT, split_axis=0, concat_axis=0, tiled=True)  29.7 us
    all_to_all x1, starting transfers between devices, exchange(): lax.all_to_all(x, CONTEXT, split_axis=0, concat_axis=0, tiled=True)  17.6 us
    ppermute x1, starting transfers between devices, on_device(): swapped = lax.ppermute(theirs, 'core', [(0, 1), (1, 0)])  14.9 us
  transfers between devices with their start and end apart: 2, of which 2 were waited for; matrix products, arithmetic and copies ran while one was open for 0% of the time, Pallas kernels for 2%

profile of v5, /device:TPU:1, one launch (start us, length us, event | category | flops | bytes accessed | tf_op | source)
XLA Modules:
  0.0 188.1 jit_solution(16628013329750743900)
XLA Ops:
  0.6 2.2 %gate.1 = f32[1088,128]{1,0:T(8,128)} custom-call(s32[1]{0:T(128)} %bitcast.1.wait_ref.core_ref, f32[128,512]{1,0:T(8,128)} %q_ref.1, f32[128,512]{1,0:T(8,128)} %k_hbm.1, f32[128,512]{1,0:T(8,128)} %v_hbm.1, f32[128,512]{1,0:T(8,128)} %z_hbm.1, f32[32,128]{1,0:T(8,128)} %bitcast.11), custom_call_target="tpu_custom_call" | custom-call | tf_op jit(solution)/shard_map/gate/pallas_call | solution.py:52
  2.9 76.6 %all_to_all.15 = f32[64,1,2176]{2,1,0:T(1,128)S(1)} all-to-all(f32[64,1,2176]{2,1,0:T(1,128)} %bitcast.10), channel_id=1, replica_groups=mesh['y'=4,'xh'=2,'core'=2,'xl'=2,'z'=32] {'xl','z'}, dimensions={0} | all-to-all | bytes 1114112 | tf_op jit(solution)/shard_map/all_to_all | solution.py:286
  79.5 3.2 %conv.1.after_ref = f32[576,128]{1,0:T(8,128)} custom-call(f32[1088,128]{1,0:T(8,128)S(1)} %bitcast.8), custom_call_target="tpu_custom_call" | custom-call | tf_op jit(solution)/shard_map/conv/pallas_call | solution.py:157
  82.7 17.6 %all-to-all-start.1 = ((f32[64,1,1152]{2,1,0:T(1,128)}), f32[64,1,1152]{2,1,0:T(1,128)S(1)}, u32[]{:S(2)}, u32[]{:S(2)}) async-start(f32[64,1,1152]{2,1,0:T(1,128)} %bitcast.5), calls=%async_computation.1 | async-start | bytes 589824 | tf_op jit(solution)/shard_map/all_to_all | solution.py:286
  100.3 0.0 copy-start
  100.3 1.6 prefetch.1.ahead_ref
  101.9 29.7 %all-to-all-done.1 = f32[64,1,1152]{2,1,0:T(1,128)S(1)} async-done(((f32[64,1,1152]{2,1,0:T(1,128)}), f32[64,1,1152]{2,1,0:T(1,128)S(1)}, u32[]{:S(2)}, u32[]{:S(2)}) %all-to-all-start.1) | async-done | bytes 294944 | tf_op jit(solution)/shard_map/all_to_all | solution.py:286
  131.7 0.0 copy-done
  131.7 2.5 %theirs.1 = (f32[8,128,512]{2,1,0:T(8,128)S(1)}, bf16[128,512]{1,0:T(8,128)(2,1)S(1)}, f32[32,128]{1,0:T(8,128)}) custom-call(s32[1]{0:T(128)} %bitcast.1.wait_ref.core_ref, f32[128,512]{1,0:T(8,128)S(1)} %copy-done, f32[576,128]{1,0:T(8,128)S(1)} %bitcast.9, bf16[4,512,512]{2,1,0:T(8,128)(2,1)S(1)} %prefetch.1.ahead_ref, bf16[512,8192]{1,0:T(8,128)(2,1)} %w_hbm.5), custom_call_target="tpu_custom_call" | custom-call | flops 536870912 | bytes 4194304 | tf_op jit(solution)/shard_map/theirs/pallas_call | solution.py:251
  134.2 14.9 %collective-permute-start = (f32[8,128,512]{2,1,0:T(8,128)S(1)}, f32[8,128,512]{2,1,0:T(8,128)S(1)}, u32[]{:S(2)}, u32[]{:S(2)}) collective-permute-start(f32[8,128,512]{2,1,0:T(8,128)S(1)} %get-tuple-element.6), channel_id=1, source_target_pairs={{0,64},{64,0},{1,65},{65,1},{2,66},{66,2},{3,67},{67,3},{4,68},{68... | collective-permute-start | bytes 6291464 | tf_op jit(solution)/shard_map/ppermute | solution.py:293
  149.1 2.7 %mine.1 = f32[8,128,512]{2,1,0:T(8,128)S(1)} custom-call(s32[1]{0:T(128)} %bitcast.core_ref, bf16[128,512]{1,0:T(8,128)(2,1)S(1)} %get-tuple-element.5.mixed_ref, bf16[512,8192]{1,0:T(8,128)(2,1)} %w_hbm.5), custom_call_target="tpu_custom_call" | custom-call | flops 536870912 | bytes 4194304 | tf_op jit(solution)/shard_map/mine/pallas_call | solution.py:265
  151.8 1.1 collective-permute-done
  152.9 0.5 add.3
  153.4 33.7 %all_to_all.16 = f32[8,128,512]{2,1,0:T(8,128)S(1)} all-to-all(f32[8,128,512]{2,1,0:T(8,128)S(1)} %add.3), channel_id=1, replica_groups=mesh['y'=4,'xh'=2,'core'=2,'xl'=2,'z'=32] {'y','xh'}, dimensions={0} | all-to-all | bytes 4194304 | tf_op jit(solution)/shard_map/all_to_all | solution.py:295
  187.1 0.9 reduce_sum.9
Async XLA Ops:
  82.7 49.0 %all-to-all-start.1 = ((f32[64,1,1152]{2,1,0:T(1,128)}), f32[64,1,1152]{2,1,0:T(1,128)S(1)}, u32[]{:S(2)}, u32[]{:S(2)}) async-start(f32[64,1,1152]{2,1,0:T(1,128)} %bitcast.5), calls=%async_computation.1 | async-start | bytes 589824 | tf_op jit(solution)/shard_map/all_to_all | solution.py:286
  100.3 31.4 %copy-start = (f32[128,512]{1,0:T(8,128)S(1)}, f32[128,512]{1,0:T(8,128)}, u32[]{:S(2)}) copy-start(f32[128,512]{1,0:T(8,128)} %q_ref.1) | copy-start | bytes 786436
  134.2 18.7 %collective-permute-start = (f32[8,128,512]{2,1,0:T(8,128)S(1)}, f32[8,128,512]{2,1,0:T(8,128)S(1)}, u32[]{:S(2)}, u32[]{:S(2)}) collective-permute-start(f32[8,128,512]{2,1,0:T(8,128)S(1)} %get-tuple-element.6), channel_id=1, source_target_pairs={{0,64},{64,0},{1,65},{65,1},{2,66},{66,2},{3,67},{67,3},{4,68},{68... | collective-permute-start | bytes 6291464 | tf_op jit(solution)/shard_map/ppermute | solution.py:293

commit v6 on v5

--- a/solution.py
+++ b/solution.py
@@ -16,7 +16,7 @@
 VMEM = pl.BlockSpec(memory_space=pltpu.VMEM)
 HBM = pl.BlockSpec(memory_space=pltpu.HBM)
 SMEM = pl.BlockSpec(memory_space=pltpu.SMEM)
-LATER_NS = 12000
+LATER_NS = 19000
 
 
 def params(mib):

time: 188 us -> 185 us (0.984)
  blocking collectives: 110 us -> 105 us
  starting transfers between devices: 32.6 us -> 35.2 us
    all_to_all x1, blocking collectives: 76.6 us -> 71.3 us  [exchange(): lax.all_to_all(x, CONTEXT, split_axis=0, concat_axis=0, tiled=True)]
    ppermute x1, starting transfers between devices: 14.9 us -> 19.7 us  [on_device(): swapped = lax.ppermute(theirs, 'core', [(0, 1), (1, 0)])]
    all_to_all x1, starting transfers between devices: 17.6 us -> 15.6 us  [exchange(): lax.all_to_all(x, CONTEXT, split_axis=0, concat_axis=0, tiled=True)]
where the time goes in v6:
time: 185 us
  blocking collectives  105 us (57%)
  starting transfers between devices  35.2 us (19%)
  waiting for transfers between devices  30.1 us (16%)
  Pallas kernels  12.2 us (7%)
    all_to_all x1, blocking collectives, exchange(): lax.all_to_all(x, CONTEXT, split_axis=0, concat_axis=0, tiled=True)  71.3 us
    all_to_all x1, blocking collectives, on_device(): lax.all_to_all(summed, ('y', 'xh'), split_axis=0, concat_axis=0, tiled=True)  33.7 us
    all_to_all x1, waiting for transfers between devices, exchange(): lax.all_to_all(x, CONTEXT, split_axis=0, concat_axis=0, tiled=True)  29.1 us
    ppermute x1, starting transfers between devices, on_device(): swapped = lax.ppermute(theirs, 'core', [(0, 1), (1, 0)])  19.7 us
    all_to_all x1, starting transfers between devices, exchange(): lax.all_to_all(x, CONTEXT, split_axis=0, concat_axis=0, tiled=True)  15.6 us
  transfers between devices with their start and end apart: 2, of which 2 were waited for; matrix products, arithmetic and copies ran while one was open for 0% of the time, Pallas kernels for 2%

profile of v6, /device:TPU:1, one launch (start us, length us, event | category | flops | bytes accessed | tf_op | source)
XLA Modules:
  0.0 184.7 jit_solution(5124013509846337192)
XLA Ops:
  0.6 2.2 %gate.1 = f32[1088,128]{1,0:T(8,128)} custom-call(s32[1]{0:T(128)} %bitcast.1.wait_ref.core_ref, f32[128,512]{1,0:T(8,128)} %q_ref.1, f32[128,512]{1,0:T(8,128)} %k_hbm.1, f32[128,512]{1,0:T(8,128)} %v_hbm.1, f32[128,512]{1,0:T(8,128)} %z_hbm.1, f32[32,128]{1,0:T(8,128)} %bitcast.11), custom_call_target="tpu_custom_call" | custom-call | tf_op jit(solution)/shard_map/gate/pallas_call | solution.py:52
  2.9 71.3 %all_to_all.15 = f32[64,1,2176]{2,1,0:T(1,128)S(1)} all-to-all(f32[64,1,2176]{2,1,0:T(1,128)} %bitcast.10), channel_id=1, replica_groups=mesh['y'=4,'xh'=2,'core'=2,'xl'=2,'z'=32] {'xl','z'}, dimensions={0} | all-to-all | bytes 1114112 | tf_op jit(solution)/shard_map/all_to_all | solution.py:286
  74.1 3.2 %conv.1.after_ref = f32[576,128]{1,0:T(8,128)} custom-call(f32[1088,128]{1,0:T(8,128)S(1)} %bitcast.8), custom_call_target="tpu_custom_call" | custom-call | tf_op jit(solution)/shard_map/conv/pallas_call | solution.py:157
  77.3 15.6 %all-to-all-start.1 = ((f32[64,1,1152]{2,1,0:T(1,128)}), f32[64,1,1152]{2,1,0:T(1,128)S(1)}, u32[]{:S(2)}, u32[]{:S(2)}) async-start(f32[64,1,1152]{2,1,0:T(1,128)} %bitcast.5), calls=%async_computation.1 | async-start | bytes 589824 | tf_op jit(solution)/shard_map/all_to_all | solution.py:286
  92.9 0.0 copy-start
  92.9 1.6 prefetch.1.ahead_ref
  94.5 29.1 %all-to-all-done.1 = f32[64,1,1152]{2,1,0:T(1,128)S(1)} async-done(((f32[64,1,1152]{2,1,0:T(1,128)}), f32[64,1,1152]{2,1,0:T(1,128)S(1)}, u32[]{:S(2)}, u32[]{:S(2)}) %all-to-all-start.1) | async-done | bytes 294944 | tf_op jit(solution)/shard_map/all_to_all | solution.py:286
  123.6 0.0 copy-done
  123.6 2.5 %theirs.1 = (f32[8,128,512]{2,1,0:T(8,128)S(1)}, bf16[128,512]{1,0:T(8,128)(2,1)S(1)}, f32[32,128]{1,0:T(8,128)}) custom-call(s32[1]{0:T(128)} %bitcast.1.wait_ref.core_ref, f32[128,512]{1,0:T(8,128)S(1)} %copy-done, f32[576,128]{1,0:T(8,128)S(1)} %bitcast.9, bf16[4,512,512]{2,1,0:T(8,128)(2,1)S(1)} %prefetch.1.ahead_ref, bf16[512,8192]{1,0:T(8,128)(2,1)} %w_hbm.5), custom_call_target="tpu_custom_call" | custom-call | flops 536870912 | bytes 4194304 | tf_op jit(solution)/shard_map/theirs/pallas_call | solution.py:251
  126.1 19.7 %collective-permute-start = (f32[8,128,512]{2,1,0:T(8,128)S(1)}, f32[8,128,512]{2,1,0:T(8,128)S(1)}, u32[]{:S(2)}, u32[]{:S(2)}) collective-permute-start(f32[8,128,512]{2,1,0:T(8,128)S(1)} %get-tuple-element.6), channel_id=1, source_target_pairs={{0,64},{64,0},{1,65},{65,1},{2,66},{66,2},{3,67},{67,3},{4,68},{68... | collective-permute-start | bytes 6291464 | tf_op jit(solution)/shard_map/ppermute | solution.py:293
  145.8 2.7 %mine.1 = f32[8,128,512]{2,1,0:T(8,128)S(1)} custom-call(s32[1]{0:T(128)} %bitcast.core_ref, bf16[128,512]{1,0:T(8,128)(2,1)S(1)} %get-tuple-element.5.mixed_ref, bf16[512,8192]{1,0:T(8,128)(2,1)} %w_hbm.5), custom_call_target="tpu_custom_call" | custom-call | flops 536870912 | bytes 4194304 | tf_op jit(solution)/shard_map/mine/pallas_call | solution.py:265
  148.5 1.1 collective-permute-done
  149.6 0.5 add.3
  150.1 33.7 %all_to_all.16 = f32[8,128,512]{2,1,0:T(8,128)S(1)} all-to-all(f32[8,128,512]{2,1,0:T(8,128)S(1)} %add.3), channel_id=1, replica_groups=mesh['y'=4,'xh'=2,'core'=2,'xl'=2,'z'=32] {'y','xh'}, dimensions={0} | all-to-all | bytes 4194304 | tf_op jit(solution)/shard_map/all_to_all | solution.py:295
  183.8 0.9 reduce_sum.9
Async XLA Ops:
  77.3 46.3 %all-to-all-start.1 = ((f32[64,1,1152]{2,1,0:T(1,128)}), f32[64,1,1152]{2,1,0:T(1,128)S(1)}, u32[]{:S(2)}, u32[]{:S(2)}) async-start(f32[64,1,1152]{2,1,0:T(1,128)} %bitcast.5), calls=%async_computation.1 | async-start | bytes 589824 | tf_op jit(solution)/shard_map/all_to_all | solution.py:286
  92.9 30.7 %copy-start = (f32[128,512]{1,0:T(8,128)S(1)}, f32[128,512]{1,0:T(8,128)}, u32[]{:S(2)}) copy-start(f32[128,512]{1,0:T(8,128)} %q_ref.1) | copy-start | bytes 786436
  126.1 23.4 %collective-permute-start = (f32[8,128,512]{2,1,0:T(8,128)S(1)}, f32[8,128,512]{2,1,0:T(8,128)S(1)}, u32[]{:S(2)}, u32[]{:S(2)}) collective-permute-start(f32[8,128,512]{2,1,0:T(8,128)S(1)} %get-tuple-element.6), channel_id=1, source_target_pairs={{0,64},{64,0},{1,65},{65,1},{2,66},{66,2},{3,67},{67,3},{4,68},{68... | collective-permute-start | bytes 6291464 | tf_op jit(solution)/shard_map/ppermute | solution.py:293

commit v7 on v6

--- a/solution.py
+++ b/solution.py
@@ -16,7 +16,7 @@
 VMEM = pl.BlockSpec(memory_space=pltpu.VMEM)
 HBM = pl.BlockSpec(memory_space=pltpu.HBM)
 SMEM = pl.BlockSpec(memory_space=pltpu.SMEM)
-LATER_NS = 19000
+LATER_NS = 24000
 
 
 def params(mib):

time: 185 us -> 187 us (1.011)
    ppermute x1, starting transfers between devices: 19.7 us -> 29.2 us  [on_device(): swapped = lax.ppermute(theirs, 'core', [(0, 1), (1, 0)])]
    all_to_all x1, starting transfers between devices: 15.6 us -> 7.53 us  [exchange(): lax.all_to_all(x, CONTEXT, split_axis=0, concat_axis=0, tiled=True)]
where the time goes in v7:
time: 187 us; the launch traced here: 186 us
  blocking collectives  105 us (56%)
  starting transfers between devices  36.7 us (20%)
  waiting for transfers between devices  30.3 us (16%)
  Pallas kernels  12.2 us (7%)
    all_to_all x1, blocking collectives, exchange(): lax.all_to_all(x, CONTEXT, split_axis=0, concat_axis=0, tiled=True)  71.3 us
    all_to_all x1, blocking collectives, on_device(): lax.all_to_all(summed, ('y', 'xh'), split_axis=0, concat_axis=0, tiled=True)  33.7 us
    all_to_all x1, waiting for transfers between devices, exchange(): lax.all_to_all(x, CONTEXT, split_axis=0, concat_axis=0, tiled=True)  29.3 us
    ppermute x1, starting transfers between devices, on_device(): swapped = lax.ppermute(theirs, 'core', [(0, 1), (1, 0)])  29.2 us
    all_to_all x1, starting transfers between devices, exchange(): lax.all_to_all(x, CONTEXT, split_axis=0, concat_axis=0, tiled=True)  7.53 us
  transfers between devices with their start and end apart: 2, of which 2 were waited for; matrix products, arithmetic and copies ran while one was open for 0% of the time, Pallas kernels for 2%

profile of v7, /device:TPU:1, one launch (start us, length us, event | category | flops | bytes accessed | tf_op | source)
XLA Modules:
  0.0 186.5 jit_solution(4321948199550762612)
XLA Ops:
  0.6 2.2 %gate.1 = f32[1088,128]{1,0:T(8,128)} custom-call(s32[1]{0:T(128)} %bitcast.1.wait_ref.core_ref, f32[128,512]{1,0:T(8,128)} %q_ref.1, f32[128,512]{1,0:T(8,128)} %k_hbm.1, f32[128,512]{1,0:T(8,128)} %v_hbm.1, f32[128,512]{1,0:T(8,128)} %z_hbm.1, f32[32,128]{1,0:T(8,128)} %bitcast.11), custom_call_target="tpu_custom_call" | custom-call | tf_op jit(solution)/shard_map/gate/pallas_call | solution.py:52
  2.9 71.3 %all_to_all.15 = f32[64,1,2176]{2,1,0:T(1,128)S(1)} all-to-all(f32[64,1,2176]{2,1,0:T(1,128)} %bitcast.10), channel_id=1, replica_groups=mesh['y'=4,'xh'=2,'core'=2,'xl'=2,'z'=32] {'xl','z'}, dimensions={0} | all-to-all | bytes 1114112 | tf_op jit(solution)/shard_map/all_to_all | solution.py:286
  74.2 3.2 %conv.1.after_ref = f32[576,128]{1,0:T(8,128)} custom-call(f32[1088,128]{1,0:T(8,128)S(1)} %bitcast.8), custom_call_target="tpu_custom_call" | custom-call | tf_op jit(solution)/shard_map/conv/pallas_call | solution.py:157
  77.3 7.5 %all-to-all-start.1 = ((f32[64,1,1152]{2,1,0:T(1,128)}), f32[64,1,1152]{2,1,0:T(1,128)S(1)}, u32[]{:S(2)}, u32[]{:S(2)}) async-start(f32[64,1,1152]{2,1,0:T(1,128)} %bitcast.5), calls=%async_computation.1 | async-start | bytes 589824 | tf_op jit(solution)/shard_map/all_to_all | solution.py:286
  84.9 0.0 copy-start
  84.9 1.6 prefetch.1.ahead_ref
  86.5 29.3 %all-to-all-done.1 = f32[64,1,1152]{2,1,0:T(1,128)S(1)} async-done(((f32[64,1,1152]{2,1,0:T(1,128)}), f32[64,1,1152]{2,1,0:T(1,128)S(1)}, u32[]{:S(2)}, u32[]{:S(2)}) %all-to-all-start.1) | async-done | bytes 294944 | tf_op jit(solution)/shard_map/all_to_all | solution.py:286
  115.8 0.0 copy-done
  115.8 2.5 %theirs.1 = (f32[8,128,512]{2,1,0:T(8,128)S(1)}, bf16[128,512]{1,0:T(8,128)(2,1)S(1)}, f32[32,128]{1,0:T(8,128)}) custom-call(s32[1]{0:T(128)} %bitcast.1.wait_ref.core_ref, f32[128,512]{1,0:T(8,128)S(1)} %copy-done, f32[576,128]{1,0:T(8,128)S(1)} %bitcast.9, bf16[4,512,512]{2,1,0:T(8,128)(2,1)S(1)} %prefetch.1.ahead_ref, bf16[512,8192]{1,0:T(8,128)(2,1)} %w_hbm.5), custom_call_target="tpu_custom_call" | custom-call | flops 536870912 | bytes 4194304 | tf_op jit(solution)/shard_map/theirs/pallas_call | solution.py:251
  118.3 29.2 %collective-permute-start = (f32[8,128,512]{2,1,0:T(8,128)S(1)}, f32[8,128,512]{2,1,0:T(8,128)S(1)}, u32[]{:S(2)}, u32[]{:S(2)}) collective-permute-start(f32[8,128,512]{2,1,0:T(8,128)S(1)} %get-tuple-element.6), channel_id=1, source_target_pairs={{0,64},{64,0},{1,65},{65,1},{2,66},{66,2},{3,67},{67,3},{4,68},{68... | collective-permute-start | bytes 6291464 | tf_op jit(solution)/shard_map/ppermute | solution.py:293
  147.5 2.7 %mine.1 = f32[8,128,512]{2,1,0:T(8,128)S(1)} custom-call(s32[1]{0:T(128)} %bitcast.core_ref, bf16[128,512]{1,0:T(8,128)(2,1)S(1)} %get-tuple-element.5.mixed_ref, bf16[512,8192]{1,0:T(8,128)(2,1)} %w_hbm.5), custom_call_target="tpu_custom_call" | custom-call | flops 536870912 | bytes 4194304 | tf_op jit(solution)/shard_map/mine/pallas_call | solution.py:265
  150.3 1.1 collective-permute-done
  151.3 0.5 add.3
  151.8 33.7 %all_to_all.16 = f32[8,128,512]{2,1,0:T(8,128)S(1)} all-to-all(f32[8,128,512]{2,1,0:T(8,128)S(1)} %add.3), channel_id=1, replica_groups=mesh['y'=4,'xh'=2,'core'=2,'xl'=2,'z'=32] {'y','xh'}, dimensions={0} | all-to-all | bytes 4194304 | tf_op jit(solution)/shard_map/all_to_all | solution.py:295
  185.5 0.9 reduce_sum.9
Async XLA Ops:
  77.3 38.5 %all-to-all-start.1 = ((f32[64,1,1152]{2,1,0:T(1,128)}), f32[64,1,1152]{2,1,0:T(1,128)S(1)}, u32[]{:S(2)}, u32[]{:S(2)}) async-start(f32[64,1,1152]{2,1,0:T(1,128)} %bitcast.5), calls=%async_computation.1 | async-start | bytes 589824 | tf_op jit(solution)/shard_map/all_to_all | solution.py:286
  84.9 30.9 %copy-start = (f32[128,512]{1,0:T(8,128)S(1)}, f32[128,512]{1,0:T(8,128)}, u32[]{:S(2)}) copy-start(f32[128,512]{1,0:T(8,128)} %q_ref.1) | copy-start | bytes 786436
  118.3 33.0 %collective-permute-start = (f32[8,128,512]{2,1,0:T(8,128)S(1)}, f32[8,128,512]{2,1,0:T(8,128)S(1)}, u32[]{:S(2)}, u32[]{:S(2)}) collective-permute-start(f32[8,128,512]{2,1,0:T(8,128)S(1)} %get-tuple-element.6), channel_id=1, source_target_pairs={{0,64},{64,0},{1,65},{65,1},{2,66},{66,2},{3,67},{67,3},{4,68},{68... | collective-permute-start | bytes 6291464 | tf_op jit(solution)/shard_map/ppermute | solution.py:293
